TPU v7x, 512 devices: a whole 4x4x16 slice. The times are simulated.
512 devices in a mesh: mp: 8 (over z_lo, core), feat: 64 (over x, z_hi, y).
Axes of the slice: x: 4, y: 4, z: 16 (z_hi: 4, z_lo: 4; z = z_hi * 4 + z_lo), core: 2. Of those that a mesh axis runs over, the one named last changes fastest.
Arguments:
- target_ids: int32 [16], replicated, may hold values from 0 to 127999
- target_pos: int32 [16], replicated, may hold values from 24 to 47
- unembed: bfloat16 [128000, 2304], P(('mp', 'feat')), may hold values from -6 to 6
- attn_weights: float32 [8, 16, 48, 48], P('mp'), may hold values from 0.02 to 1
- inv_rms: float32 [16, 48], replicated, may hold values from 0.5 to 2
- norm_gain: float32 [2304], replicated, may hold values from 0.1 to 1.9
- w_value: bfloat16 [4, 2304, 256], P(None, 'mp'), may hold values from -0.125 to 0.125
- w_out: bfloat16 [8, 256, 2304], P('mp'), may hold values from -0.375 to 0.375
- decoder: bfloat16 [2, 98304, 2304], P(None, ('mp', 'feat')), may hold values from -0.125 to 0.125
- activation: bfloat16 [16, 48, 98304], P(None, None, ('mp', 'feat')), may hold values from 0.5 to 4
- active: int32 [16, 48, 98304], P(None, None, ('mp', 'feat')), may hold values 0 or 1
Outputs:
- attribution: float32 [16, 48, 98304], P(None, None, ('mp', 'feat'))
All inputs are finite; a program needn't handle non-finite values. No bound on the sum of `active` on one device may be relied on, other than what follows from the above.
Results may differ from a plain program's by a relative error of at most 0.0035.
Values may be sent and summed in bfloat16 or wider, within the bound.
No kernel may reach another device: no remote copies, remote signals or barrier semaphores. Data moves between devices by JAX's collectives and lax.ppermute only.
A program may use at most 64 MiB of HBM per device.

v0:
```python
import jax
import jax.numpy as jnp
from jax import lax
from jax.sharding import PartitionSpec as P


def on_device(
    target_ids,
    target_pos,
    unembed,
    attn_weights,
    inv_rms,
    norm_gain,
    w_value,
    w_out,
    decoder,
    activation,
    active,
):
    vocab_rows = unembed.shape[0]
    model_width = unembed.shape[1]
    targets = target_ids.shape[0]
    positions = inv_rms.shape[1]
    local_heads = w_out.shape[0]
    kv_heads = w_value.shape[0]
    column_count = w_value.shape[1]
    row_count = targets * positions
    own_rows = row_count // lax.axis_size("feat")
    device_rank = lax.axis_index("mp") * lax.axis_size("feat") + lax.axis_index("feat")
    first_row = device_rank * vocab_rows
    picker = (
        target_ids[:, None] == first_row + jnp.arange(vocab_rows, dtype=jnp.int32)[None, :]
    ).astype(jnp.bfloat16)
    direction = lax.psum(
        jnp.dot(picker, unembed, preferred_element_type=jnp.float32), ("mp", "feat")
    )
    placing = (jnp.arange(positions, dtype=jnp.int32)[None, :] == target_pos[:, None]).astype(
        jnp.float32
    )
    upper = (placing[:, :, None] * direction[:, None, :]).reshape(row_count, model_width)
    lowered_top = upper.astype(jnp.bfloat16)
    row_start = lax.axis_index("feat") * own_rows
    column_start = lax.axis_index("mp") * column_count
    index_pos = jnp.arange(positions, dtype=jnp.int32)
    causal = (index_pos[:, None] >= index_pos[None, :]).astype(jnp.float32)
    weights = attn_weights * causal
    pattern = weights / jnp.sum(weights, axis=-1, keepdims=True)
    flipped = jnp.swapaxes(pattern, 2, 3).reshape(local_heads, row_count, positions)
    own_pattern = lax.dynamic_slice_in_dim(flipped, row_start, own_rows, 1)
    row_group = (row_start + jnp.arange(own_rows, dtype=jnp.int32)) // positions
    group_pick = (row_group[:, None] == jnp.arange(targets, dtype=jnp.int32)[None, :]).astype(
        jnp.float32
    )
    block_pattern = (own_pattern[:, :, None, :] * group_pick[None, :, :, None]).reshape(
        local_heads, own_rows, row_count
    )
    mixed = jnp.einsum(
        "hrq,qd->hrd",
        block_pattern,
        lowered_top.astype(jnp.float32),
        precision=lax.Precision.HIGHEST,
    ).astype(jnp.bfloat16)
    spread = jnp.einsum("hrd,hkd->hrk", mixed, w_out, preferred_element_type=jnp.float32).astype(
        jnp.bfloat16
    )
    all_spread = lax.all_gather(spread, "mp", axis=0, tiled=True)
    group_size = local_heads * lax.axis_size("mp") // kv_heads
    value_heads = jnp.repeat(w_value, group_size, axis=0)
    heads_sum = jnp.einsum(
        "hrk,hck->rc", all_spread, value_heads, preferred_element_type=jnp.float32
    )
    upper_rows = lax.dynamic_slice_in_dim(upper, row_start, own_rows, 0)
    upper_block = lax.dynamic_slice_in_dim(upper_rows, column_start, column_count, 1)
    scale_rows = lax.dynamic_slice_in_dim(inv_rms.reshape(row_count, 1), row_start, own_rows, 0)
    gain_columns = lax.dynamic_slice_in_dim(norm_gain, column_start, column_count, 0)
    below_block = upper_block + scale_rows * gain_columns[None, :] * heads_sum
    lowered_block = below_block.astype(jnp.bfloat16)
    top_scores = jnp.einsum(
        "rd,fd->rf", lowered_top, decoder[1], preferred_element_type=jnp.float32
    )
    tall_block = lax.all_gather(lowered_block, "feat", axis=0, tiled=True)
    lowered_bottom = lax.all_gather(tall_block, "mp", axis=1, tiled=True)
    bottom_scores = jnp.einsum(
        "rd,fd->rf", lowered_bottom, decoder[0], preferred_element_type=jnp.float32
    )
    scores = bottom_scores + top_scores
    feature_count = decoder.shape[1]
    attribution = (
        activation.astype(jnp.float32).reshape(row_count, feature_count)
        * active.reshape(row_count, feature_count).astype(jnp.float32)
        * scores
    )
    return attribution.reshape(targets, positions, feature_count)


def solution(mesh):
    in_specs = (
        P(),
        P(),
        P(("mp", "feat"), None),
        P("mp", None, None, None),
        P(),
        P(),
        P(None, "mp", None),
        P("mp", None, None),
        P(None, ("mp", "feat"), None),
        P(None, None, ("mp", "feat")),
        P(None, None, ("mp", "feat")),
    )
    out_specs = P(None, None, ("mp", "feat"))
    return jax.shard_map(
        on_device, mesh=mesh, in_specs=in_specs, out_specs=out_specs, check_vma=False
    )
```

profile of v0, /device:TPU:1, one launch (start us, length us, event | category | flops | bytes accessed | tf_op | source)
XLA Modules:
  0.0 759.5 jit_solution(12552327615252992566)
XLA Ops:
  6.5 0.0 copy-start
  6.5 0.0 copy-start.7
  6.5 0.0 copy-start.6
  6.5 0.0 all-reduce.2.cloned.1.call-start
  6.6 1.2 copy-done
  7.8 0.0 copy-start.1
  7.8 1.7 fusion.23
  9.5 0.0 all-reduce.2.cloned.1.call-update
  9.6 0.0 all-gather.5.cloned.1.call-start
  9.7 1.2 multiply_reduce_fusion
  10.8 1.2 divide_bitcast_fusion
  12.0 0.1 copy.21
  12.1 0.2 reshape.175
  12.3 0.1 constant_dynamic-slice_fusion
  12.4 0.1 copy.22
  12.5 0.0 copy-done.7
  12.5 0.1 fusion.27
  12.6 0.1 reshape.179
  12.7 0.0 copy-done.6
  12.7 0.1 reshape.174
  12.7 0.8 dynamic_slice.15
  13.5 0.1 dynamic-slice
  13.6 0.1 dynamic-slice_bitcast_fusion
  13.7 452.4 %all-reduce.2.cloned.1.call-done = f32[16,2304]{1,0:T(8,128)} async-done(((f32[16,2304]{1,0:T(8,128)}), f32[16,2304]{1,0:T(8,128)}) %all-reduce.2.cloned.1.call-update) | async-done | bytes 147472 | tf_op jit(solution)/shard_map/psum | solution.py:34
  466.0 2.9 fusion
  468.9 0.0 copy-done.1
  468.9 0.4 fusion.11
  469.3 13.9 %all-gather.1 = bf16[8,12,256]{2,1,0:T(8,128)(2,1)S(1)} all-gather(bf16[1,12,256]{2,1,0:T(8,128)(2,1)S(1)} %fusion.11), channel_id=2, replica_groups=mesh['mp'=8,'feat'=64] {'mp'}, dimensions={0}, use_global_device_ids=true | all-gather | bytes 55296 | tf_op jit(solution)/shard_map/all_gather | solution.py:66
  483.1 0.0 copy-done.4
  483.2 0.5 mul.102
  483.7 0.0 copy-start.2
  483.7 0.5 copy-done.3
  484.2 0.1 broadcast_in_dim.2
  484.3 0.4 fusion.7
  484.7 195.3 %all-gather.2 = bf16[64,12,288]{2,1,0:T(8,128)(2,1)S(1)} all-gather(bf16[1,12,288]{2,1,0:T(8,128)(2,1)S(1)} %fusion.7), channel_id=1, replica_groups=mesh['mp'=8,'feat'=64] {'feat'}, dimensions={0}, use_global_device_ids=true | all-gather | bytes 449280 | tf_op jit(solution)/shard_map/all_gather | solution.py:81
  680.0 0.3 reshape.184
  680.3 1.0 copy.23
  681.3 0.0 all-gather.5.cloned.1.call-update
  681.4 0.0 copy-done.2
  681.4 1.1 convert_multiply_fusion
  682.5 0.2 copy.24
  682.7 0.0 copy-start.5
  682.7 0.5 multiply_convert_fusion
  683.3 0.9 copy-done.5
  684.2 1.3 fusion.14
  685.5 62.9 %all-gather.5.cloned.1.call-done = bf16[768,2304]{0,1:T(8,128)(2,1)} async-done(((bf16[768,288]{0,1:T(8,128)(2,1)}), bf16[768,2304]{0,1:T(8,128)(2,1)}) %all-gather.5.cloned.1.call-update) | async-done | bytes 3538960 | tf_op jit(solution)/shard_map/all_gather | solution.py:82
  748.4 3.1 fusion.1
  751.5 1.1 copy.25
  (6 shorter events, 0.0 us)
Async XLA Ops:
  6.5 1.3 copy-start
  6.5 6.0 copy-start.7
  6.5 6.1 copy-start.6
  6.5 459.5 %all-reduce.2.cloned.1.call-start = ((), (), s32[]{:S(2)}) async-start(), calls=%async_computation | async-start | bytes 294912 | tf_op jit(solution)/shard_map/psum | solution.py:34
  7.8 461.1 %copy-start.1 = (bf16[1,256,2304]{2,1,0:T(8,128)(2,1)S(1)}, bf16[1,256,2304]{2,1,0:T(8,128)(2,1)}, u32[]{:S(2)}) copy-start(bf16[1,256,2304]{2,1,0:T(8,128)(2,1)} %param.18) | copy-start | bytes 3538948
  9.6 738.8 %all-gather.5.cloned.1.call-start = ((), (), s32[]{:S(2)}) async-start(), calls=%async_computation.1 | async-start | bytes 3981312 | tf_op jit(solution)/shard_map/all_gather | solution.py:82
  466.0 17.1 %copy-start.4 = (f32[16,2304]{1,0:T(8,128)S(1)}, f32[16,2304]{1,0:T(8,128)}, u32[]{:S(2)}) copy-start(f32[16,2304]{1,0:T(8,128)} %all-reduce.2.cloned.1.call-done) | copy-start | bytes 442372
  483.1 1.1 copy-start.3
  483.7 197.7 %copy-start.2 = (s32[16,48,192]{2,1,0:T(8,128)S(1)}, s32[16,48,192]{2,1,0:T(8,128)}, u32[]{:S(2)}) copy-start(s32[16,48,192]{2,1,0:T(8,128)} %param.21) | copy-start | bytes 1769476
  682.7 1.5 copy-start.5
Sparse Core Ops, SparseCore 0:
  12.8 453.1 all-reduce.1
  681.5 66.8 all-gather.4
where the time goes:
time: 761 us; the launch traced here: 759 us
  waiting for transfers between devices  515 us (68%)
  blocking collectives  209 us (27%)
  between operations  13.6 us (2%)
  matrix products  9.85 us (1%)
    psum x1, waiting for transfers between devices, on_device(): lax.psum(jnp.dot(picker, unembed, preferred_element_type=jnp.float32), ('...  452 us
    all_gather x1, blocking collectives, on_device(): tall_block = lax.all_gather(lowered_block, 'feat', axis=0, tiled=True)  195 us
    all_gather x1, waiting for transfers between devices, on_device(): lowered_bottom = lax.all_gather(tall_block, 'mp', axis=1, tiled=True)  62.9 us
  transfers between devices with their start and end apart: 2, of which 2 were waited for; matrix products, arithmetic and copies ran while one was open for 1% of the time, Pallas kernels for 0%

commit v1 on v0

v1 whole, which is shorter than its diff:
```python
import jax
import jax.numpy as jnp
from jax import lax
from jax.sharding import Mesh, PartitionSpec as P

MP = ("zl", "core")
FEAT = ("x", "zh", "y")
ALL = MP + FEAT


def spread_out(block, axes):
    members = lax.axis_size(axes)
    return lax.all_to_all(jnp.broadcast_to(block[None], (members,) + block.shape), axes, 0, 0)


def on_device(
    target_ids,
    target_pos,
    unembed,
    attn_weights,
    inv_rms,
    norm_gain,
    w_value,
    w_out,
    decoder,
    activation,
    active,
):
    vocab_rows, width = unembed.shape
    targets = target_ids.shape[0]
    positions = inv_rms.shape[1]
    kv_heads = w_value.shape[0]
    head_size = w_out.shape[1]
    heads = w_out.shape[0] * lax.axis_size(MP)
    f32 = jnp.float32
    bf16 = jnp.bfloat16

    value_all = lax.all_gather(w_value, MP, axis=1, tiled=True)

    first_row = lax.axis_index(ALL) * vocab_rows
    picker = (
        target_ids[:, None] == first_row + jnp.arange(vocab_rows, dtype=jnp.int32)[None, :]
    ).astype(bf16)
    found = jnp.dot(picker, unembed, preferred_element_type=f32).astype(bf16)
    parts = lax.all_to_all(found, ("x", "y"), 0, 0, tiled=True)
    row = jnp.sum(parts.astype(f32), axis=0).astype(bf16)
    row = jnp.sum(spread_out(row, ("zl", "zh")).astype(f32), axis=0).astype(bf16)
    pairs = spread_out(row, ("x", "y", "core"))
    direction = jnp.sum(pairs.astype(f32).reshape(targets, 2, width), axis=1).astype(bf16)

    key = jnp.arange(positions, dtype=jnp.int32)
    at_target = (key[None, :] == target_pos[:, None]).astype(f32)
    weight_row = jnp.sum(attn_weights[0] * at_target[:, :, None], axis=1)
    weight_row = jnp.where(key[None, :] <= target_pos[:, None], weight_row, 0.0)
    pattern = weight_row / jnp.sum(weight_row, axis=-1, keepdims=True)
    gradient = jnp.einsum("gd,kd->gk", direction, w_out[0], preferred_element_type=f32)
    message = jnp.concatenate(
        [gradient, pattern * inv_rms, jnp.zeros((targets, 128 - positions), f32)], axis=1
    )
    by_head = spread_out(message, MP)
    gradients = by_head[:, :, :head_size].reshape(kv_heads, heads // kv_heads * targets, head_size)
    scale = by_head[:, :, head_size : head_size + positions]

    lowered = jnp.einsum(
        "vrk,vck->vrc", gradients.astype(bf16), value_all, preferred_element_type=f32
    )
    lowered = (lowered * norm_gain[None, None, :]).astype(bf16).reshape(heads * targets, width)
    bottom = jnp.einsum(
        "rd,fd->rf",
        jnp.concatenate([lowered, direction], axis=0),
        decoder[0],
        preferred_element_type=f32,
    )
    top = jnp.einsum("rd,fd->rf", direction, decoder[1], preferred_element_type=f32)
    features = decoder.shape[1]
    per_head = bottom[: heads * targets].reshape(heads, targets, features)
    own = bottom[heads * targets :] + top
    scores = at_target[:, :, None] * own[:, None, :]
    for h in range(heads):
        scores = scores + scale[h][:, :, None] * per_head[h][:, None, :]
    return activation.astype(f32) * active.astype(f32) * scores


def solution(mesh):
    mesh = Mesh(mesh.devices.reshape(4, 2, 4, 4, 4), ALL)
    in_specs = (
        P(),
        P(),
        P(ALL, None),
        P(MP, None, None, None),
        P(),
        P(),
        P(None, MP, None),
        P(MP, None, None),
        P(None, ALL, None),
        P(None, None, ALL),
        P(None, None, ALL),
    )
    out_specs = P(None, None, ALL)
    return jax.shard_map(
        on_device, mesh=mesh, in_specs=in_specs, out_specs=out_specs, check_vma=False
    )
```

time: 761 us -> 101 us (0.13)
  waiting for transfers between devices: 515 us -> 20.6 us
  blocking collectives: 209 us -> 27.4 us
  starting transfers between devices: 0.04 us -> 22 us
    psum x1 -> x0, waiting for transfers between devices: 452 us -> none  [on_device(): lax.psum(jnp.dot(picker, unembed, preferred_element_type=jnp.float32), ('...]
    all_gather x2 -> x0, blocking collectives: 209 us -> none  [the longest x1 195 us: on_device(): tall_block = lax.all_gather(lowered_block, 'feat', axis=0, tiled=True)]
    all_gather x1, waiting for transfers between devices: 62.9 us -> 0.02 us  [on_device(): value_all = lax.all_gather(w_value, MP, axis=1, tiled=True)]
    all_to_all x0 -> x2, blocking collectives: none -> 27.4 us  [the longest x1 13.9 us: on_device(): parts = lax.all_to_all(found, ('x', 'y'), 0, 0, tiled=True)]
    all_to_all x0 -> x2, starting transfers between devices: none -> 22 us  [spread_out(): lax.all_to_all(jnp.broadcast_to(block[None], (members,) + block.shape), a...]
    all_to_all x0 -> x2, waiting for transfers between devices: none -> 19.8 us  [spread_out(): lax.all_to_all(jnp.broadcast_to(block[None], (members,) + block.shape), a...]
  transfers between devices with their start and end apart: 2 -> 3, of which waited for: 2 -> 2; matrix products, arithmetic and copies ran while one was open for 1% -> 9% of each run, Pallas kernels for 0% -> 0%
where the time goes in v1:
time: 101 us; the launch traced here: 100 us
  blocking collectives  27.4 us (27%)
  starting transfers between devices  22 us (22%)
  waiting for transfers between devices  20.6 us (20%)
  between operations  13.7 us (14%)
  other arithmetic  6.99 us (7%)
  matrix products  6.06 us (6%)
  local copies, waits for them, and re-layouts  3.55 us (4%)
    all_to_all x2, starting transfers between devices, spread_out(): lax.all_to_all(jnp.broadcast_to(block[None], (members,) + block.shape), a...  22 us
    all_to_all x2, waiting for transfers between devices, spread_out(): lax.all_to_all(jnp.broadcast_to(block[None], (members,) + block.shape), a...  19.8 us
    all_to_all x1, blocking collectives, on_device(): parts = lax.all_to_all(found, ('x', 'y'), 0, 0, tiled=True)  13.9 us
    all_to_all x1, blocking collectives, spread_out(): lax.all_to_all(jnp.broadcast_to(block[None], (members,) + block.shape), a...  13.5 us
    dot_general x1, matrix products, on_device(): jnp.einsum('vrk,vck->vrc', gradients.astype(bf16), value_all, preferred_e...  3.95 us
    unnamed x24, local copies, waits for them, and re-layouts  2.55 us
    broadcast_in_dim x2, other arithmetic, spread_out(): jnp.broadcast_to(block[None], (members,) + block.shape)  2.47 us
  transfers between devices with their start and end apart: 3, of which 2 were waited for; matrix products, arithmetic and copies ran while one was open for 9% of the time, Pallas kernels for 0%

profile of v1, /device:TPU:1, one launch (start us, length us, event | category | flops | bytes accessed | tf_op | source)
XLA Modules:
  0.0 100.2 jit_solution(2918440003667930035)
XLA Ops:
  6.5 0.0 copy-start
  6.5 0.0 all-gather.2.cloned.1.call-start
  6.5 0.7 all-gather.2.cloned.1.call-update
  7.3 0.5 copy-done
  7.8 1.0 %fusion.1 = bf16[16,1,2304]{2,0,1:T(8,128)(2,1)S(1)} fusion(bf16[250,2304]{1,0:T(8,128)(2,1)S(1)} %copy-done, s32[250]{0:T(256)S(1)} %iota_add_fusion, s32[16]{0:T(128)} %param.11), kind=kOutput, calls=%fused_computation.3 | convolution fusion | flops 18472864 | bytes 1226792 | tf_op jit(solution)/shard_map/dot_general | solution.py:44
  8.8 0.5 broadcast.41
  9.3 0.6 reduce.6
  9.9 13.9 %all_to_all.29 = bf16[16,2,1152]{2,1,0:T(2,128)(2,1)S(1)} all-to-all(bf16[16,2,1152]{2,1,0:T(2,128)(2,1)S(1)} %reshape.88), channel_id=1, replica_groups=mesh['zl'=4,'core'=2,'x'=4,'zh'=4,'y'=4] {'x','y'}, dimensions={0} | all-to-all | bytes 147456 | tf_op jit(solution)/shard_map/all_to_all | solution.py:45
  23.8 0.1 reshape.89
  23.9 0.1 reduce_sum.54
  24.0 0.1 broadcast_in_dim.11
  24.1 0.0 copy-start.7
  24.1 1.0 reduce.7
  25.1 0.7 reshape.90
  25.8 14.9 %all-to-all-start.1 = ((bf16[16,2,1152]{2,1,0:T(2,128)(2,1)}), bf16[16,2,1152]{2,1,0:T(2,128)(2,1)S(1)}, u32[]{:S(2)}, u32[]{:S(2)}) async-start(bf16[16,2,1152]{2,1,0:T(2,128)(2,1)} %reshape.90), calls=%async_computation.1 | async-start | bytes 147456 | tf_op jit(solution)/shard_map/all_to_all | solution.py:13
  40.7 0.1 fusion.16
  40.8 0.1 pad.4.clone
  40.9 0.2 fusion.12
  41.0 0.2 fusion.18
  41.2 12.0 %all-to-all-done.1 = bf16[16,2,1152]{2,1,0:T(2,128)(2,1)S(1)} async-done(((bf16[16,2,1152]{2,1,0:T(2,128)(2,1)}), bf16[16,2,1152]{2,1,0:T(2,128)(2,1)S(1)}, u32[]{:S(2)}, u32[]{:S(2)}) %all-to-all-start.1) | async-done | bytes 73760 | tf_op jit(solution)/shard_map/all_to_all | solution.py:13
  53.2 0.1 reshape.91
  53.3 0.1 reduce_sum.55
  53.4 0.0 copy-start.1
  53.4 0.2 broadcast_in_dim.12
  53.6 1.5 %reduce.8 = bf16[32,2304]{1,0:T(8,128)(2,1)S(1)} reduce(bf16[32,1,2304]{2,1,0:T(2,128)(2,1)S(1)} %broadcast_in_dim.12, bf16[]{:T(256)} %broadcast.41), dimensions={1}, to_apply=%broadcast_in_dim.12.reduce_sub_computation | reduce | bytes 294914 | tf_op jit(solution)/shard_map/broadcast_in_dim | solution.py:13
  55.1 0.7 reshape.92
  55.8 7.0 %all-to-all-start.2 = ((bf16[32,2,1152]{2,1,0:T(2,128)(2,1)}), bf16[32,2,1152]{2,1,0:T(2,128)(2,1)S(1)}, u32[]{:S(2)}, u32[]{:S(2)}) async-start(bf16[32,2,1152]{2,1,0:T(2,128)(2,1)} %reshape.92), calls=%async_computation.2 | async-start | bytes 294912 | tf_op jit(solution)/shard_map/all_to_all | solution.py:13
  62.9 0.1 divide_multiply_fusion
  62.9 7.9 %all-to-all-done.2 = bf16[32,2,1152]{2,1,0:T(2,128)(2,1)S(1)} async-done(((bf16[32,2,1152]{2,1,0:T(2,128)(2,1)}), bf16[32,2,1152]{2,1,0:T(2,128)(2,1)S(1)}, u32[]{:S(2)}, u32[]{:S(2)}) %all-to-all-start.2) | async-done | bytes 147488 | tf_op jit(solution)/shard_map/all_to_all | solution.py:13
  70.8 0.1 reshape.93
  70.9 0.9 reduce.5
  71.8 0.0 copy-start.6
  71.8 0.1 all_to_all.23
  71.8 0.4 reduce_sum.56
  72.2 0.4 fusion.2
  72.6 0.1 maximum_maximum_fusion
  72.7 13.5 %all_to_all.30 = f32[8,16,384]{2,1,0:T(8,128)S(1)} all-to-all(f32[8,16,384]{2,1,0:T(8,128)S(1)} %broadcast_in_dim.15), channel_id=1, replica_groups=mesh['zl'=4,'core'=2,'x'=4,'zh'=4,'y'=4] {'zl','core'}, dimensions={0} | all-to-all | bytes 393216 | tf_op jit(solution)/shard_map/all_to_all | solution.py:13
  86.2 0.0 all-gather.2.cloned.1.call-done
  86.2 0.0 copy-start.3
  86.3 3.9 %fusion = bf16[4,32,2304]{2,1,0:T(8,128)(2,1)S(1)} fusion(bf16[4,32,256]{2,1,0:T(8,128)(2,1)S(1)} %bitcast.39, bf16[4,2304,256]{2,1,0:T(8,128)(2,1)} %all-gather.2.cloned.1.call-done, f32[2304]{0:T(1024)S(1)} %copy-done.6), kind=kOutput, calls=%fused_computation.1 | convolution fusion | flops 151584768 | bytes 5383168 | tf_op jit(solution)/shard_map/vrk,vck->vrc/dot_general | solution.py:64
  90.2 0.0 copy-start.2
  90.2 0.0 copy-start.5
  90.2 0.4 fusion.5
  90.7 0.3 convolution_add_fusion
  91.0 0.1 fusion.20
  91.1 0.3 copy-done.2
  91.4 0.1 copy-done.5
  91.5 1.9 %add_multiply_fusion = f32[16,48,192]{2,1,0:T(8,128)} fusion(s32[16,48,192]{2,1,0:T(8,128)S(1)} %copy-done.2, bf16[16,48,192]{2,1,0:T(8,128)(2,1)S(1)} %copy-done.5, f32[16,192]{1,0:T(8,128)S(1)} %get-tuple-element.14, f32[16,48]{1,0:T(8,128)S(1)} %get-tuple-element.6, f32[16,192]{1,0:T(8,128)S(1)} %get-tuple-element.15, f32[16,48]{1,0:T(8,128)S(1)} %get-tuple-element.7, ...), kind=kLoop, calls=%fused_computation.12 | loop fusion | flops 3096576 | bytes 1612800 | tf_op jit(solution)/shard_map/mul | solution.py:81
  (14 shorter events, 0.1 us)
Async XLA Ops:
  6.5 1.3 %copy-start = (bf16[250,2304]{1,0:T(8,128)(2,1)S(1)}, bf16[250,2304]{1,0:T(8,128)(2,1)}, u32[]{:S(2)}) copy-start(bf16[250,2304]{1,0:T(8,128)(2,1)} %param.13) | copy-start | bytes 3456004
  6.5 79.7 %all-gather.2.cloned.1.call-start = ((), (), s32[]{:S(2)}) async-start(), calls=%async_computation.4 | async-start | bytes 5308416 | tf_op jit(solution)/shard_map/all_gather | solution.py:38
  7.8 32.9 %copy-start.8 = (s32[16]{0:T(128)S(1)}, s32[16]{0:T(128)}, u32[]{:S(2)}) copy-start(s32[16]{0:T(128)} %param.12) | copy-start | bytes 196
  7.8 33.1 %copy-start.4 = (f32[1,16,48,48]{3,2,1,0:T(8,128)S(1)}, f32[1,16,48,48]{3,2,1,0:T(8,128)}, u32[]{:S(2)}) copy-start(f32[1,16,48,48]{3,2,1,0:T(8,128)} %param.14) | copy-start | bytes 442372
  24.1 38.7 %copy-start.7 = (f32[16,48]{1,0:T(8,128)S(1)}, f32[16,48]{1,0:T(8,128)}, u32[]{:S(2)}) copy-start(f32[16,48]{1,0:T(8,128)} %param.15) | copy-start | bytes 9220
  25.8 27.4 %all-to-all-start.1 = ((bf16[16,2,1152]{2,1,0:T(2,128)(2,1)}), bf16[16,2,1152]{2,1,0:T(2,128)(2,1)S(1)}, u32[]{:S(2)}, u32[]{:S(2)}) async-start(bf16[16,2,1152]{2,1,0:T(2,128)(2,1)} %reshape.90), calls=%async_computation.1 | async-start | bytes 147456 | tf_op jit(solution)/shard_map/all_to_all | solution.py:13
  53.4 18.8 %copy-start.1 = (bf16[1,256,2304]{2,1,0:T(8,128)(2,1)S(1)}, bf16[1,256,2304]{2,1,0:T(8,128)(2,1)}, u32[]{:S(2)}) copy-start(bf16[1,256,2304]{2,1,0:T(8,128)(2,1)} %param.18) | copy-start | bytes 3538948
  55.8 15.0 %all-to-all-start.2 = ((bf16[32,2,1152]{2,1,0:T(2,128)(2,1)}), bf16[32,2,1152]{2,1,0:T(2,128)(2,1)S(1)}, u32[]{:S(2)}, u32[]{:S(2)}) async-start(bf16[32,2,1152]{2,1,0:T(2,128)(2,1)} %reshape.92), calls=%async_computation.2 | async-start | bytes 294912 | tf_op jit(solution)/shard_map/all_to_all | solution.py:13
  71.8 14.5 %copy-start.6 = (f32[2304]{0:T(1024)S(1)}, f32[2304]{0:T(1024)}, u32[]{:S(2)}) copy-start(f32[2304]{0:T(1024)} %param.16) | copy-start | bytes 27652
  86.2 4.0 %copy-start.3 = (bf16[2,192,2304]{2,1,0:T(8,128)(2,1)S(1)}, bf16[2,192,2304]{2,1,0:T(8,128)(2,1)}, u32[]{:S(2)}) copy-start(bf16[2,192,2304]{2,1,0:T(8,128)(2,1)} %param.19) | copy-start | bytes 5308420
  90.2 1.1 %copy-start.2 = (s32[16,48,192]{2,1,0:T(8,128)S(1)}, s32[16,48,192]{2,1,0:T(8,128)}, u32[]{:S(2)}) copy-start(s32[16,48,192]{2,1,0:T(8,128)} %param.21) | copy-start | bytes 1769476
  90.2 1.2 %copy-start.5 = (bf16[16,48,192]{2,1,0:T(8,128)(2,1)S(1)}, bf16[16,48,192]{2,1,0:T(8,128)(2,1)}, u32[]{:S(2)}) copy-start(bf16[16,48,192]{2,1,0:T(8,128)(2,1)} %param.20) | copy-start | bytes 884740
Sparse Core Ops, SparseCore 0:
  9.4 72.6 all-gather.1

commit v2 on v1

v2 whole, which is shorter than its diff:
```python
import jax
import jax.numpy as jnp
from jax import lax
from jax.sharding import Mesh, PartitionSpec as P

MP = ("zl", "core")
FEAT = ("x", "zh", "y")
ALL = MP + FEAT


def spread_out(block, axes):
    members = lax.axis_size(axes)
    return lax.all_to_all(jnp.broadcast_to(block[None], (members,) + block.shape), axes, 0, 0)


def on_device(
    target_ids,
    target_pos,
    unembed,
    attn_weights,
    inv_rms,
    norm_gain,
    w_value,
    w_out,
    decoder,
    activation,
    active,
):
    vocab_rows, width = unembed.shape
    targets = target_ids.shape[0]
    positions = inv_rms.shape[1]
    kv_heads = w_value.shape[0]
    heads = w_out.shape[0] * lax.axis_size(MP)
    group_size = heads // kv_heads
    f32 = jnp.float32
    bf16 = jnp.bfloat16

    first_row = lax.axis_index(ALL) * vocab_rows
    wanted = jnp.repeat(target_ids, 2)
    picker = (
        wanted[:, None] == first_row + jnp.arange(vocab_rows, dtype=jnp.int32)[None, :]
    ).astype(bf16)
    found = jnp.dot(picker, unembed, preferred_element_type=f32).astype(bf16)
    parts = lax.all_to_all(found, ("x", "y", "core"), 0, 0, tiled=True)
    row = jnp.sum(parts.astype(f32), axis=0).astype(bf16)
    row = jnp.sum(spread_out(row, ("zl", "zh")).astype(f32), axis=0).astype(bf16)[None]

    target = lax.axis_index(("x", "y"))
    here = lax.dynamic_index_in_dim(target_pos, target, 0)
    key = jnp.arange(positions, dtype=jnp.int32)[None]
    weight_row = lax.dynamic_slice(
        attn_weights, (0, target, here[0], 0), (1, 1, 1, positions)
    ).reshape(1, positions)
    weight_row = jnp.where(key <= here[:, None], weight_row, 0.0)
    scale = weight_row / jnp.sum(weight_row, axis=-1, keepdims=True)
    scale = scale * lax.dynamic_slice_in_dim(inv_rms, target, 1, 0)
    high = scale.astype(bf16)
    low = (scale - high.astype(f32)).astype(bf16)
    gap = jnp.zeros((1, 64 - positions), bf16)
    gradient = jnp.einsum("gd,kd->gk", row, w_out[0], preferred_element_type=f32).astype(bf16)
    message = jnp.concatenate([gradient, high, gap, low, gap], axis=1)
    heard = spread_out(message, MP).reshape(heads, w_out.shape[1] + 128)
    head_size = w_out.shape[1]
    lowered = jnp.einsum(
        "vjk,vck->vjc",
        heard[:, :head_size].reshape(kv_heads, group_size, head_size),
        w_value,
        preferred_element_type=f32,
    )
    columns = w_value.shape[1]
    gain = lax.dynamic_slice_in_dim(norm_gain, lax.axis_index(MP) * columns, columns, 0)
    lowered = (lowered * gain).astype(bf16).reshape(heads, columns)
    blocks = spread_out(lowered, MP)
    lowered = jnp.swapaxes(blocks, 0, 1).reshape(heads, width)
    own_row = jnp.pad(row.reshape(heads, columns), ((0, 0), (0, 384 - columns)))
    by_head = jnp.concatenate([lowered, heard[:, head_size:], own_row], axis=1)
    by_target = spread_out(by_head, ("x", "y"))

    direction = by_target[:, :, width + 128 : width + 128 + columns].reshape(targets, width)

    features = decoder.shape[1]
    own = jnp.einsum("rd,fd->rf", direction, decoder[0], preferred_element_type=f32)
    own = own + jnp.einsum("rd,fd->rf", direction, decoder[1], preferred_element_type=f32)
    per_head = jnp.einsum(
        "rd,fd->rf",
        by_target[:, :, :width].reshape(targets * heads, width),
        decoder[0],
        preferred_element_type=f32,
    ).reshape(targets, heads, features)
    scale = by_target[:, :, width : width + positions].astype(f32)
    scale = scale + by_target[:, :, width + 64 : width + 64 + positions].astype(f32)
    at_target = (key == target_pos[:, None]).astype(f32)
    scores = at_target[:, :, None] * own[:, None, :]
    for h in range(heads):
        scores = scores + scale[:, h, :, None] * per_head[:, h, None, :]
    return activation.astype(f32) * active.astype(f32) * scores


def solution(mesh):
    mesh = Mesh(mesh.devices.reshape(4, 2, 4, 4, 4), ALL)
    in_specs = (
        P(),
        P(),
        P(ALL, None),
        P(MP, None, None, None),
        P(),
        P(),
        P(None, MP, None),
        P(MP, None, None),
        P(None, ALL, None),
        P(None, None, ALL),
        P(None, None, ALL),
    )
    out_specs = P(None, None, ALL)
    return jax.shard_map(
        on_device, mesh=mesh, in_specs=in_specs, out_specs=out_specs, check_vma=False
    )
```

time: 101 us -> 95.4 us (0.945)
  between operations: 13.7 us -> 2.21 us
  blocking collectives: 27.4 us -> 17.6 us
  waiting for transfers between devices: 20.6 us -> 26.4 us
  starting transfers between devices: 22 us -> 27.3 us
  local copies, waits for them, and re-layouts: 3.55 us -> 8.14 us
  matrix products: 6.06 us -> 3.28 us
  other arithmetic: 6.99 us -> 9.69 us
    all_to_all x2 -> x1, blocking collectives: 27.4 us -> 17.6 us  [on_device(): parts = lax.all_to_all(found, ('x', 'y', 'core'), 0, 0, tiled=True)]
    all_to_all x2 -> x4, waiting for transfers between devices: 19.8 us -> 26.4 us  [spread_out(): lax.all_to_all(jnp.broadcast_to(block[None], (members,) + block.shape), a...]
    all_to_all x2 -> x4, starting transfers between devices: 22 us -> 27.3 us  [spread_out(): lax.all_to_all(jnp.broadcast_to(block[None], (members,) + block.shape), a...]
    dot_general x3 -> x4, matrix products: 4.77 us -> 2.56 us  [the longest x1 1.64 us: on_device(): jnp.einsum('rd,fd->rf', by_target[:, :, :width].reshape(targets * heads,...]
    convert_element_type x1 -> x3, other arithmetic: 0.07 us -> 2.03 us  [the longest x1 1.95 us: on_device(): low = (scale - high.astype(f32)).astype(bf16)]
    dynamic_slice x0 -> x2, local copies, waits for them, and re-layouts: none -> 1.42 us  [the longest x1 0.77 us: on_device(): lax.dynamic_slice_in_dim(norm_gain, lax.axis_index(MP) * columns, columns...]
    broadcast_in_dim x3 -> x5, local copies, waits for them, and re-layouts: 0.25 us -> 1.66 us  [spread_out(): jnp.broadcast_to(block[None], (members,) + block.shape)]
    reduce_sum x3 -> x1, other arithmetic: 0.74 us -> 1.96 us  [on_device(): scale = weight_row / jnp.sum(weight_row, axis=-1, keepdims=True)]
  transfers between devices with their start and end apart: 3 -> 4, of which waited for: 2 -> 4; matrix products, arithmetic and copies ran while one was open for 9% -> 6% of each run, Pallas kernels for 0% -> 0%
where the time goes in v2:
time: 95.4 us; the launch traced here: 94.6 us
  starting transfers between devices  27.3 us (29%)
  waiting for transfers between devices  26.4 us (28%)
  blocking collectives  17.6 us (18%)
  other arithmetic  9.69 us (10%)
  local copies, waits for them, and re-layouts  8.14 us (9%)
  matrix products  3.28 us (3%)
  between operations  2.21 us (2%)
    all_to_all x4, starting transfers between devices, spread_out(): lax.all_to_all(jnp.broadcast_to(block[None], (members,) + block.shape), a...  27.3 us
    all_to_all x4, waiting for transfers between devices, spread_out(): lax.all_to_all(jnp.broadcast_to(block[None], (members,) + block.shape), a...  26.4 us
    all_to_all x1, blocking collectives, on_device(): parts = lax.all_to_all(found, ('x', 'y', 'core'), 0, 0, tiled=True)  17.6 us
    unnamed x25, local copies, waits for them, and re-layouts  2.09 us
    reduce_sum x1, other arithmetic, on_device(): scale = weight_row / jnp.sum(weight_row, axis=-1, keepdims=True)  1.96 us
    convert_element_type x1, other arithmetic, on_device(): low = (scale - high.astype(f32)).astype(bf16)  1.95 us
  transfers between devices with their start and end apart: 4, of which 4 were waited for; matrix products, arithmetic and copies ran while one was open for 6% of the time, Pallas kernels for 0%

profile of v2, /device:TPU:1, one launch (start us, length us, event | category | flops | bytes accessed | tf_op | source)
XLA Modules:
  0.0 94.6 jit_solution(14222648683888143034)
XLA Ops:
  0.0 0.8 broadcast_in_dim.18
  0.8 0.1 eq.35
  0.9 0.4 copy-done
  1.3 0.3 fusion
  1.6 0.6 broadcast.72
  2.2 0.7 reduce.6
  2.9 17.6 %all_to_all.30 = bf16[32,2,1152]{2,1,0:T(2,128)(2,1)S(1)} all-to-all(bf16[32,2,1152]{2,1,0:T(2,128)(2,1)S(1)} %reshape.119), channel_id=1, replica_groups=mesh['zl'=4,'core'=2,'x'=4,'zh'=4,'y'=4] {'x','y','core'}, dimensions={0} | all-to-all | bytes 294912 | tf_op jit(solution)/shard_map/all_to_all | solution.py:44
  20.5 0.1 reshape.120
  20.6 0.3 reduce_sum.33
  20.9 0.1 broadcast_in_dim.19
  21.0 1.1 %reduce.7 = bf16[16,2304]{1,0:T(8,128)(2,1)S(1)} reduce(bf16[16,1,2304]{2,1,0:T(2,128)(2,1)S(1)} %broadcast_in_dim.19, bf16[]{:T(256)} %broadcast.72), dimensions={1}, to_apply=%broadcast_in_dim.19.reduce_sub_computation | reduce | bytes 147458 | tf_op jit(solution)/shard_map/broadcast_in_dim | solution.py:13
  22.1 0.7 reshape.121
  22.7 13.7 %all-to-all-start.1 = ((bf16[16,2,1152]{2,1,0:T(2,128)(2,1)}), bf16[16,2,1152]{2,1,0:T(2,128)(2,1)S(1)}, u32[]{:S(2)}, u32[]{:S(2)}) async-start(bf16[16,2,1152]{2,1,0:T(2,128)(2,1)} %reshape.121), calls=%async_computation.1 | async-start | bytes 147456 | tf_op jit(solution)/shard_map/all_to_all | solution.py:13
  36.4 0.7 dynamic_slice.13
  39.0 2.0 %fusion.19 = f32[]{:T(128)} fusion(f32[1,16,48,48]{3,2,1,0:T(8,128)} %param.14, s32[]{:T(128)S(6)} %select_n.28, s32[]{:T(128)S(6)} %select_n.29, s32[]{:T(128)} %bitcast.3), kind=kLoop, calls=%fused_computation.39 | loop fusion | flops 143 | bytes 208 | tf_op jit(solution)/shard_map/reduce_sum | solution.py:55
  41.0 2.0 %subtract_convert_fusion = (bf16[1,48]{1,0:T(2,128)(2,1)S(1)}, bf16[1,48]{1,0:T(2,128)(2,1)S(1)}) fusion(f32[16,48]{1,0:T(8,128)} %param.15, s32[]{:T(128)S(6)} %select_n.28, f32[]{:T(128)} %fusion.19, f32[1,16,48,48]{3,2,1,0:T(8,128)} %param.14, s32[]{:T(128)S(6)} %select_n.29, s32[]{:T(128)} %bitcast.3), kind=kLoop, calls=%fused_computation.38 | loop fusion | flops 432 | bytes 592 | tf_op jit(solution)/shard_map/convert_element_type | solution.py:58
  42.9 5.3 %all-to-all-done.1 = bf16[16,2,1152]{2,1,0:T(2,128)(2,1)S(1)} async-done(((bf16[16,2,1152]{2,1,0:T(2,128)(2,1)}), bf16[16,2,1152]{2,1,0:T(2,128)(2,1)S(1)}, u32[]{:S(2)}, u32[]{:S(2)}) %all-to-all-start.1) | async-done | bytes 73760 | tf_op jit(solution)/shard_map/all_to_all | solution.py:13
  48.2 0.1 reshape.122
  48.2 0.1 reduce_sum.34
  48.4 0.0 copy-done.2
  48.4 0.4 fusion.1
  48.9 0.1 concatenate.6
  49.0 0.7 reduce.8
  49.7 0.7 reshape.123
  50.4 5.3 %all-to-all-start.2 = ((bf16[8,2,192]{2,1,0:T(2,128)(2,1)}), bf16[8,2,192]{2,1,0:T(2,128)(2,1)S(1)}, u32[]{:S(2)}, u32[]{:S(2)}) async-start(bf16[8,2,192]{2,1,0:T(2,128)(2,1)} %reshape.123), calls=%async_computation.2 | async-start | bytes 16384 | tf_op jit(solution)/shard_map/all_to_all | solution.py:13
  55.7 0.8 dynamic_slice.16
  56.5 4.2 %all-to-all-done.2 = bf16[8,2,192]{2,1,0:T(2,128)(2,1)S(1)} async-done(((bf16[8,2,192]{2,1,0:T(2,128)(2,1)}), bf16[8,2,192]{2,1,0:T(2,128)(2,1)S(1)}, u32[]{:S(2)}, u32[]{:S(2)}) %all-to-all-start.2) | async-done | bytes 6176 | tf_op jit(solution)/shard_map/all_to_all | solution.py:13
  60.7 0.1 reshape.124
  60.8 0.3 fusion.3
  61.1 0.6 broadcast_in_dim.24
  61.7 4.0 %all-to-all-start.3 = ((bf16[8,8,288]{2,1,0:T(8,128)(2,1)}), bf16[8,8,288]{2,1,0:T(8,128)(2,1)S(1)}, u32[]{:S(2)}, u32[]{:S(2)}) async-start(bf16[8,8,288]{2,1,0:T(8,128)(2,1)} %broadcast_in_dim.24), calls=%async_computation.3 | async-start | bytes 98304 | tf_op jit(solution)/shard_map/all_to_all | solution.py:13
  65.7 0.1 reshape_broadcast_in_dim.3
  65.8 5.0 %all-to-all-done.3 = bf16[8,8,288]{2,1,0:T(8,128)(2,1)S(1)} async-done(((bf16[8,8,288]{2,1,0:T(8,128)(2,1)}), bf16[8,8,288]{2,1,0:T(8,128)(2,1)S(1)}, u32[]{:S(2)}, u32[]{:S(2)}) %all-to-all-start.3) | async-done | bytes 36896 | tf_op jit(solution)/shard_map/all_to_all | solution.py:13
  70.7 0.1 reshape.113
  70.8 0.0 copy-start.1
  70.9 0.9 broadcast_in_dim.25
  71.8 4.3 %all-to-all-start.4 = ((bf16[16,8,2816]{2,1,0:T(8,128)(2,1)}), bf16[16,8,2816]{2,1,0:T(8,128)(2,1)}, u32[]{:S(2)}, u32[]{:S(2)}) async-start(bf16[16,8,2816]{2,1,0:T(8,128)(2,1)} %broadcast_in_dim.25), calls=%async_computation.4 | async-start | bytes 1441792 | tf_op jit(solution)/shard_map/all_to_all | solution.py:13
  76.0 0.1 fusion.18
  76.1 12.1 %all-to-all-done.4 = bf16[16,8,2816]{2,1,0:T(8,128)(2,1)} async-done(((bf16[16,8,2816]{2,1,0:T(8,128)(2,1)}), bf16[16,8,2816]{2,1,0:T(8,128)(2,1)}, u32[]{:S(2)}, u32[]{:S(2)}) %all-to-all-start.4) | async-done | bytes 720928 | tf_op jit(solution)/shard_map/all_to_all | solution.py:13
  88.2 0.9 slice.99
  89.1 0.1 reshape.114
  89.2 0.3 fusion.7
  89.5 0.4 convolution_add_fusion
  89.9 0.0 copy-start.5
  89.9 1.6 %fusion.4 = f32[16,8,192]{2,1,0:T(8,128)S(1)} fusion(bf16[2,192,2304]{2,1,0:T(8,128)(2,1)S(1)} %copy-done.1, bf16[16,8,2816]{2,1,0:T(8,128)(2,1)} %all-to-all-done.4), kind=kOutput, calls=%fused_computation.7 | convolution fusion | flops 113246208 | bytes 1572864 | tf_op jit(solution)/shard_map/rd,fd->rf/dot_general | solution.py:84
  91.6 0.1 fusion.20
  91.7 0.9 convert_add_fusion
  92.7 1.9 %add_multiply_fusion = f32[16,48,192]{2,1,0:T(8,128)} fusion(s32[16,48,192]{2,1,0:T(8,128)S(1)} %copy-done.3, bf16[16,48,192]{2,1,0:T(8,128)(2,1)S(1)} %copy-done.5, f32[16,192]{1,0:T(8,128)S(1)} %get-tuple-element.23, f32[16,48]{1,0:T(8,128)S(1)} %bitcast.59, f32[16,192]{1,0:T(8,128)S(1)} %get-tuple-element.24, f32[16,48]{1,0:T(8,128)S(1)} %bitcast.60, ...), kind=kLoop, calls=%fused_computation.13 | loop fusion | flops 3096576 | bytes 1612800 | tf_op jit(solution)/shard_map/mul | solution.py:96
  (30 shorter events, 0.3 us)
Async XLA Ops:
  0.0 1.3 %copy-start = (bf16[250,2304]{1,0:T(8,128)(2,1)S(1)}, bf16[250,2304]{1,0:T(8,128)(2,1)}, u32[]{:S(2)}) copy-start(bf16[250,2304]{1,0:T(8,128)(2,1)} %param.13) | copy-start | bytes 3456004
  1.6 34.8 %copy-start.6 = (s32[16]{0:T(128)S(1)}, s32[16]{0:T(128)}, u32[]{:S(2)}) copy-start(s32[16]{0:T(128)} %param.12) | copy-start | bytes 196
  2.9 45.5 %copy-start.2 = (bf16[1,256,2304]{2,1,0:T(8,128)(2,1)S(1)}, bf16[1,256,2304]{2,1,0:T(8,128)(2,1)}, u32[]{:S(2)}) copy-start(bf16[1,256,2304]{2,1,0:T(8,128)(2,1)} %param.18) | copy-start | bytes 3538948
  20.9 39.9 %copy-start.4 = (bf16[4,288,256]{2,1,0:T(8,128)(2,1)S(1)}, bf16[4,288,256]{2,1,0:T(8,128)(2,1)}, u32[]{:S(2)}) copy-start(bf16[4,288,256]{2,1,0:T(8,128)(2,1)} %param.17) | copy-start | bytes 1769476
  22.7 25.4 %all-to-all-start.1 = ((bf16[16,2,1152]{2,1,0:T(2,128)(2,1)}), bf16[16,2,1152]{2,1,0:T(2,128)(2,1)S(1)}, u32[]{:S(2)}, u32[]{:S(2)}) async-start(bf16[16,2,1152]{2,1,0:T(2,128)(2,1)} %reshape.121), calls=%async_computation.1 | async-start | bytes 147456 | tf_op jit(solution)/shard_map/all_to_all | solution.py:13
  50.4 10.3 %all-to-all-start.2 = ((bf16[8,2,192]{2,1,0:T(2,128)(2,1)}), bf16[8,2,192]{2,1,0:T(2,128)(2,1)S(1)}, u32[]{:S(2)}, u32[]{:S(2)}) async-start(bf16[8,2,192]{2,1,0:T(2,128)(2,1)} %reshape.123), calls=%async_computation.2 | async-start | bytes 16384 | tf_op jit(solution)/shard_map/all_to_all | solution.py:13
  61.7 9.0 %all-to-all-start.3 = ((bf16[8,8,288]{2,1,0:T(8,128)(2,1)}), bf16[8,8,288]{2,1,0:T(8,128)(2,1)S(1)}, u32[]{:S(2)}, u32[]{:S(2)}) async-start(bf16[8,8,288]{2,1,0:T(8,128)(2,1)} %broadcast_in_dim.24), calls=%async_computation.3 | async-start | bytes 98304 | tf_op jit(solution)/shard_map/all_to_all | solution.py:13
  70.8 18.4 %copy-start.1 = (bf16[2,192,2304]{2,1,0:T(8,128)(2,1)S(1)}, bf16[2,192,2304]{2,1,0:T(8,128)(2,1)}, u32[]{:S(2)}) copy-start(bf16[2,192,2304]{2,1,0:T(8,128)(2,1)} %param.19) | copy-start | bytes 5308420
  71.8 16.4 %all-to-all-start.4 = ((bf16[16,8,2816]{2,1,0:T(8,128)(2,1)}), bf16[16,8,2816]{2,1,0:T(8,128)(2,1)}, u32[]{:S(2)}, u32[]{:S(2)}) async-start(bf16[16,8,2816]{2,1,0:T(8,128)(2,1)} %broadcast_in_dim.25), calls=%async_computation.4 | async-start | bytes 1441792 | tf_op jit(solution)/shard_map/all_to_all | solution.py:13
  89.9 2.8 %copy-start.3 = (s32[16,48,192]{2,1,0:T(8,128)S(1)}, s32[16,48,192]{2,1,0:T(8,128)}, u32[]{:S(2)}) copy-start(s32[16,48,192]{2,1,0:T(8,128)} %param.21) | copy-start | bytes 1769476
  89.9 2.8 %copy-start.5 = (bf16[16,48,192]{2,1,0:T(8,128)(2,1)S(1)}, bf16[16,48,192]{2,1,0:T(8,128)(2,1)}, u32[]{:S(2)}) copy-start(bf16[16,48,192]{2,1,0:T(8,128)(2,1)} %param.20) | copy-start | bytes 884740

commit v3 on v1

v3 whole, which is shorter than its diff:
```python
import functools

import jax
import jax.numpy as jnp
from jax import lax
from jax.experimental import pallas as pl
from jax.experimental.pallas import tpu as pltpu
from jax.sharding import Mesh, PartitionSpec as P

MP = ("zl", "core")
FEAT = ("x", "zh", "y")
ALL = MP + FEAT
LANES = 128
F32 = jnp.float32
BF16 = jnp.bfloat16
NT = (((1,), (1,)), ((), ()))
VMEM = pl.BlockSpec(memory_space=pltpu.VMEM)
SMEM = pl.BlockSpec(memory_space=pltpu.SMEM)


def call(body, shapes, in_specs, name):
    return pl.pallas_call(
        body,
        out_shape=shapes,
        in_specs=in_specs,
        out_specs=jax.tree.map(lambda _: VMEM, shapes),
        name=name,
        compiler_params=pltpu.CompilerParams(vmem_limit_bytes=32 * 1024 * 1024),
    )


def shape(dims, kind):
    return jax.ShapeDtypeStruct(dims, kind)


def pick_rows(ids, first, unembed, out):
    targets = ids.shape[0]
    rows, width = unembed.shape
    index = lax.broadcasted_iota(jnp.int32, (targets, rows), 0)
    wanted = jnp.zeros((targets, rows), jnp.int32)
    for g in range(targets):
        wanted = jnp.where(index == g, ids[g] - first[0], wanted)
    picker = (wanted == lax.broadcasted_iota(jnp.int32, (targets, rows), 1)).astype(BF16)
    found = jnp.dot(picker, unembed[...], preferred_element_type=F32)
    for g in range(targets):
        row = jnp.concatenate(
            [found[g : g + 1, k * LANES : (k + 1) * LANES] for k in range(width // LANES)], axis=0
        ).astype(BF16)
        out[2 * g] = row
        out[2 * g + 1] = row


def total(parts):
    value = parts[0].astype(F32)
    for i in range(1, parts.shape[0]):
        value = value + parts[i].astype(F32)
    return value


def sum_and_repeat(parts, out):
    row = total(parts).astype(BF16)
    for i in range(out.shape[0]):
        out[i] = row


def query_gradient(position, target, parts, w_out, attn, inv_rms, row_out, out):
    row = total(parts)
    row_out[...] = row.astype(BF16)
    flat = jnp.concatenate([row[k : k + 1, :] for k in range(row.shape[0])], axis=1).astype(BF16)
    gradient = lax.dot_general(flat, w_out[...], NT, preferred_element_type=F32)
    here = position[target[0]]
    weights = attn[target[0], pl.ds(here, 1), :]
    key = lax.broadcasted_iota(jnp.int32, weights.shape, 1)
    weights = jnp.where(key <= here, weights, 0.0)
    scale = weights / jnp.sum(weights, axis=1, keepdims=True)
    scale = scale * inv_rms[pl.ds(target[0], 1), :]
    positions = weights.shape[1]
    for i in range(out.shape[0]):
        for k in range(gradient.shape[1] // LANES):
            out[i, k : k + 1, :] = gradient[:, k * LANES : (k + 1) * LANES]
        out[i, 2:3, 0:positions] = scale
        out[i, 2:3, positions:] = jnp.zeros((1, LANES - positions), F32)


def lower_block(heard, w_value, gain, out):
    heads = heard.shape[0]
    kv_heads, columns, _ = w_value.shape
    gradient = jnp.concatenate([heard[:, 0, :], heard[:, 1, :]], axis=1).astype(BF16)
    head = lax.broadcasted_iota(jnp.int32, (heads, columns), 0)
    lowered = jnp.zeros((heads, columns), F32)
    for v in range(kv_heads):
        value = lax.dot_general(gradient, w_value[v], NT, preferred_element_type=F32)
        lowered = jnp.where(head // (heads // kv_heads) == v, value, lowered)
    lowered = (lowered * gain[...]).astype(BF16)
    for i in range(out.shape[0]):
        out[i] = lowered


def build_message(blocks, heard, row, out):
    heads = heard.shape[0]
    members = blocks.shape[0]
    width = members * blocks.shape[2]
    lowered = jnp.concatenate([blocks[i].astype(F32) for i in range(members)], axis=1)
    scale = heard[:, 2, :]
    high = scale.astype(BF16).astype(F32)
    low = scale - high
    both = (high + pltpu.roll(low, LANES // 2, 1)).astype(BF16)
    lowered = lowered.astype(BF16)
    rows = row[...].astype(F32)
    count = rows.shape[0]
    for i in range(out.shape[0]):
        out[i, :, 0:width] = lowered
        out[i, :, width : width + LANES] = both
    for j in range(-(-count // heads)):
        some = rows[j * heads : min((j + 1) * heads, count)]
        if some.shape[0] < heads:
            some = jnp.concatenate([some, jnp.zeros((heads - some.shape[0], LANES), F32)], axis=0)
        some = some.astype(BF16)
        start = width + (j + 1) * LANES
        for i in range(out.shape[0]):
            out[i, :, start : start + LANES] = some


def score(position, message, decoder, activation, active, out):
    targets, heads, _ = message.shape
    _, features, width = decoder.shape
    positions = activation.shape[1]
    count = width // LANES
    chunks = message[:, :, width + LANES :].astype(F32)
    direction = jnp.concatenate(
        [
            chunks[:, k % heads, (k // heads) * LANES : (k // heads + 1) * LANES]
            for k in range(count)
        ],
        axis=1,
    ).astype(BF16)
    own = lax.dot_general(direction, decoder[0], NT, preferred_element_type=F32)
    own = own + lax.dot_general(direction, decoder[1], NT, preferred_element_type=F32)
    lowered = message[:, :, 0:width].reshape(targets * heads, width)
    per_head = lax.dot_general(lowered, decoder[0], NT, preferred_element_type=F32)
    scale = message[:, :, width : width + LANES].astype(F32)
    key = lax.broadcasted_iota(jnp.int32, (heads, LANES), 1)
    first = lax.broadcasted_iota(jnp.int32, (heads, LANES), 0) == 0
    spare = jnp.zeros((heads - 1, features), F32)
    for g in range(targets):
        both = scale[g] + pltpu.roll(scale[g], LANES // 2, 1)
        here = jnp.where(first & (key == position[g]), 1.0, 0.0)
        left = jnp.concatenate([both, here], axis=0)[:, 0:positions]
        right = jnp.concatenate(
            [per_head[g * heads : (g + 1) * heads], own[g : g + 1], spare], axis=0
        )
        scores = lax.dot_general(
            left,
            right,
            (((0,), (0,)), ((), ())),
            precision=lax.Precision.HIGHEST,
            preferred_element_type=F32,
        )
        out[g] = activation[g].astype(F32) * active[g].astype(F32) * scores


def on_device(
    target_ids,
    target_pos,
    unembed,
    attn_weights,
    inv_rms,
    norm_gain,
    w_value,
    w_out,
    decoder,
    activation,
    active,
):
    vocab_rows, width = unembed.shape
    targets = target_ids.shape[0]
    tiles = width // LANES
    columns = w_value.shape[1]
    heads = lax.axis_size(MP)
    first_row = (lax.axis_index(ALL) * vocab_rows).reshape(1)
    target = lax.axis_index(("x", "y")).reshape(1)
    gain = lax.dynamic_slice_in_dim(norm_gain, lax.axis_index(MP) * columns, columns, 0)[None]

    found = call(
        pick_rows, shape((2 * targets, tiles, LANES), BF16), [SMEM, SMEM, VMEM], "pick_rows"
    )(target_ids, first_row, unembed)
    parts = lax.all_to_all(found, ("x", "y", "core"), 0, 0, tiled=True)
    ring = lax.axis_size(("zl", "zh"))
    parts = call(sum_and_repeat, shape((ring, tiles, LANES), BF16), [VMEM], "sum_and_repeat")(parts)
    parts = lax.all_to_all(parts, ("zl", "zh"), 0, 0, tiled=True)
    row, asked = call(
        query_gradient,
        (shape((tiles, LANES), BF16), shape((heads, 8, LANES), F32)),
        [SMEM, SMEM, VMEM, VMEM, VMEM, VMEM],
        "query_gradient",
    )(target_pos, target, parts, w_out[0], attn_weights[0], inv_rms)
    heard = lax.all_to_all(asked, MP, 0, 0, tiled=True)
    blocks = call(
        lower_block, shape((heads, heads, columns), BF16), [VMEM, VMEM, VMEM], "lower_block"
    )(heard, w_value, gain)
    blocks = lax.all_to_all(blocks, MP, 0, 0, tiled=True)
    length = width + LANES + -(-tiles // heads) * LANES
    message = call(
        build_message, shape((targets, heads, length), BF16), [VMEM, VMEM, VMEM], "build_message"
    )(blocks, heard, row)
    message = lax.all_to_all(message, ("x", "y"), 0, 0, tiled=True)
    return call(score, shape(activation.shape, F32), [SMEM, VMEM, VMEM, VMEM, VMEM], "score")(
        target_pos, message, decoder, activation, active
    )


def solution(mesh):
    mesh = Mesh(mesh.devices.reshape(4, 2, 4, 4, 4), ALL)
    in_specs = (
        P(),
        P(),
        P(ALL, None),
        P(MP, None, None, None),
        P(),
        P(),
        P(None, MP, None),
        P(MP, None, None),
        P(None, ALL, None),
        P(None, None, ALL),
        P(None, None, ALL),
    )
    out_specs = P(None, None, ALL)
    return jax.shard_map(
        on_device, mesh=mesh, in_specs=in_specs, out_specs=out_specs, check_vma=False
    )
```

time: 101 us -> 87 us (0.86)
  between operations: 13.7 us -> 0.08 us
  blocking collectives: 27.4 us -> 41 us
  other arithmetic: 6.99 us -> 0 us
  Pallas kernels: 0 us -> 6.94 us
  matrix products: 6.06 us -> 0 us
  waiting for transfers between devices: 20.6 us -> 16.1 us
  starting transfers between devices: 22 us -> 19.7 us
    all_to_all x2 -> x3, blocking collectives: 27.4 us -> 41 us  [the longest x1 17.9 us: on_device(): parts = lax.all_to_all(found, ('x', 'y', 'core'), 0, 0, tiled=True)]
    pallas_call x0 -> x6, Pallas kernels: none -> 6.94 us  [the longest x1 3.44 us: on_device(): call(score, shape(activation.shape, F32), [SMEM, VMEM, VMEM, VMEM, VMEM],...]
    dot_general x5 -> x0, matrix products: 6.06 us -> none  [the longest x1 3.95 us: on_device(): jnp.einsum('vrk,vck->vrc', gradients.astype(bf16), value_all, preferred_e...]
    all_to_all x2, waiting for transfers between devices: 19.8 us -> 16.1 us  [the longest x1 11.9 us: on_device(): parts = lax.all_to_all(parts, ('zl', 'zh'), 0, 0, tiled=True)]
    broadcast_in_dim x2 -> x0, other arithmetic: 2.47 us -> none  [spread_out(): jnp.broadcast_to(block[None], (members,) + block.shape)]
    all_to_all x2, starting transfers between devices: 22 us -> 19.7 us  [the longest x1 13.7 us: on_device(): parts = lax.all_to_all(parts, ('zl', 'zh'), 0, 0, tiled=True)]
    mul x2 -> x0, other arithmetic: 1.94 us -> none  [the longest x1 1.86 us: on_device(): return activation.astype(f32) * active.astype(f32) * scores]
    all_to_all x2 -> x0, other arithmetic: 1.41 us -> none  [the longest x1 0.85 us: spread_out(): lax.all_to_all(jnp.broadcast_to(block[None], (members,) + block.shape), a...]
  transfers between devices with their start and end apart: 3 -> 2, of which waited for: 2 -> 2; matrix products, arithmetic and copies ran while one was open for 9% -> 1% of each run, Pallas kernels for 0% -> 0%
where the time goes in v3:
time: 87 us; the launch traced here: 86.6 us
  blocking collectives  41 us (47%)
  starting transfers between devices  19.7 us (23%)
  waiting for transfers between devices  16.1 us (19%)
  Pallas kernels  6.94 us (8%)
  local copies, waits for them, and re-layouts  2.76 us (3%)
    all_to_all x1, blocking collectives, on_device(): parts = lax.all_to_all(found, ('x', 'y', 'core'), 0, 0, tiled=True)  17.9 us
    all_to_all x1, blocking collectives, on_device(): message = lax.all_to_all(message, ('x', 'y'), 0, 0, tiled=True)  14.7 us
    all_to_all x1, starting transfers between devices, on_device(): parts = lax.all_to_all(parts, ('zl', 'zh'), 0, 0, tiled=True)  13.7 us
    all_to_all x1, waiting for transfers between devices, on_device(): parts = lax.all_to_all(parts, ('zl', 'zh'), 0, 0, tiled=True)  11.9 us
    all_to_all x1, blocking collectives, on_device(): blocks = lax.all_to_all(blocks, MP, 0, 0, tiled=True)  8.29 us
    all_to_all x1, starting transfers between devices, on_device(): heard = lax.all_to_all(asked, MP, 0, 0, tiled=True)  6.05 us
    all_to_all x1, waiting for transfers between devices, on_device(): heard = lax.all_to_all(asked, MP, 0, 0, tiled=True)  4.19 us
    pallas_call x1, Pallas kernels, on_device(): call(score, shape(activation.shape, F32), [SMEM, VMEM, VMEM, VMEM, VMEM],...  3.44 us
  transfers between devices with their start and end apart: 2, of which 2 were waited for; matrix products, arithmetic and copies ran while one was open for 1% of the time, Pallas kernels for 0%

profile of v3, /device:TPU:1, one launch (start us, length us, event | category | flops | bytes accessed | tf_op | source)
XLA Modules:
  0.0 86.6 jit_solution(15773679246999884109)
XLA Ops:
  0.0 0.0 copy-start.8
  0.0 0.0 copy-start.7
  0.0 0.0 copy-start.1
  0.0 1.3 %copy-done.1 = bf16[250,2304]{1,0:T(8,128)(2,1)S(1)} copy-done((bf16[250,2304]{1,0:T(8,128)(2,1)S(1)}, bf16[250,2304]{1,0:T(8,128)(2,1)}, u32[]{:S(2)}) %copy-start.1) | copy-done | bytes 1152024
  1.3 0.0 copy-start.9
  1.3 0.7 copy-done.9
  2.0 0.0 copy-start.2
  2.0 0.0 copy-start.6
  2.0 0.8 pick_rows.1
  2.8 17.9 %all_to_all.25.parts = bf16[32,18,128]{2,1,0:T(8,128)(2,1)S(1)} all-to-all(bf16[32,18,128]{2,1,0:T(8,128)(2,1)S(1)} %pick_rows.1), channel_id=1, replica_groups=mesh['zl'=4,'core'=2,'x'=4,'zh'=4,'y'=4] {'x','y','core'}, dimensions={0} | all-to-all | bytes 294912 | tf_op jit(solution)/shard_map/all_to_all | solution.py:187
  20.8 0.0 copy-start.4
  20.8 0.7 sum_and_repeat.1
  21.4 13.7 %all-to-all-start.1 = ((bf16[16,18,128]{2,1,0:T(8,128)(2,1)}), bf16[16,18,128]{2,1,0:T(8,128)(2,1)S(1)}, u32[]{:S(2)}, u32[]{:S(2)}) async-start(bf16[16,18,128]{2,1,0:T(8,128)(2,1)} %sum_and_repeat.1), calls=%async_computation.1 | async-start | bytes 196608 | tf_op jit(solution)/shard_map/all_to_all | solution.py:190
  35.1 11.9 %all-to-all-done.1.parts = bf16[16,18,128]{2,1,0:T(8,128)(2,1)S(1)} async-done(((bf16[16,18,128]{2,1,0:T(8,128)(2,1)}), bf16[16,18,128]{2,1,0:T(8,128)(2,1)S(1)}, u32[]{:S(2)}, u32[]{:S(2)}) %all-to-all-start.1) | async-done | bytes 73760 | tf_op jit(solution)/shard_map/all_to_all | solution.py:190
  47.1 0.0 copy-done.8
  47.1 0.0 copy-done.7
  47.1 0.0 copy-done.2
  47.1 0.0 copy-done.6
  47.1 1.6 %query_gradient.1 = (bf16[18,128]{1,0:T(8,128)(2,1)S(1)}, f32[8,8,128]{2,1,0:T(8,128)}) custom-call(s32[16]{0:T(128)S(1)} %copy-done.8, s32[1]{0:T(128)} %bitcast.target, bf16[16,18,128]{2,1,0:T(8,128)(2,1)S(1)} %all-to-all-done.1.parts, bf16[256,2304]{1,0:T(8,128)(2,1)S(1)} %bitcast.4, f32[16,48,48]{2,1,0:T(8,128)S(1)} %bitcast.5, f32[16,48]{1,0:T(8,128)S(1)} %copy-done.7), custom_call_target="tpu_custom_call" | custom-call | tf_op jit(solution)/shard_map/query_gradient/pallas_call | solution.py:191
  48.7 6.0 %all-to-all-start.2 = ((f32[8,8,128]{2,1,0:T(8,128)}), f32[8,8,128]{2,1,0:T(8,128)S(1)}, u32[]{:S(2)}, u32[]{:S(2)}) async-start(f32[8,8,128]{2,1,0:T(8,128)} %get-tuple-element.7), calls=%async_computation.2 | async-start | bytes 65536 | tf_op jit(solution)/shard_map/all_to_all | solution.py:197
  54.7 0.8 dynamic_slice.3
  55.5 4.2 %all-to-all-done.2.heard = f32[8,8,128]{2,1,0:T(8,128)S(1)} async-done(((f32[8,8,128]{2,1,0:T(8,128)}), f32[8,8,128]{2,1,0:T(8,128)S(1)}, u32[]{:S(2)}, u32[]{:S(2)}) %all-to-all-start.2) | async-done | bytes 32800 | tf_op jit(solution)/shard_map/all_to_all | solution.py:197
  59.7 0.0 copy-done.4
  59.7 0.0 copy-start.3
  59.7 0.3 lower_block.1
  60.0 0.0 copy-start
  60.0 0.0 copy-start.5
  60.0 8.3 %all_to_all.26.blocks = bf16[8,8,288]{2,1,0:T(8,128)(2,1)S(1)} all-to-all(bf16[8,8,288]{2,1,0:T(8,128)(2,1)S(1)} %lower_block.1), channel_id=1, replica_groups=mesh['zl'=4,'core'=2,'x'=4,'zh'=4,'y'=4] {'zl','core'}, dimensions={0} | all-to-all | bytes 73728 | tf_op jit(solution)/shard_map/all_to_all | solution.py:201
  68.3 0.1 build_message.1
  68.4 14.7 %all_to_all.27.message = bf16[16,8,2816]{2,1,0:T(8,128)(2,1)S(1)} all-to-all(bf16[16,8,2816]{2,1,0:T(8,128)(2,1)S(1)} %build_message.1), channel_id=1, replica_groups=mesh['zl'=4,'core'=2,'x'=4,'zh'=4,'y'=4] {'x','y'}, dimensions={0} | all-to-all | bytes 1441792 | tf_op jit(solution)/shard_map/all_to_all | solution.py:206
  83.1 0.0 copy-done.3
  83.1 0.0 copy-done
  83.1 0.0 copy-done.5
  83.2 3.4 %score.1 = f32[16,48,192]{2,1,0:T(8,128)} custom-call(s32[16]{0:T(128)S(1)} %copy-done.8, bf16[16,8,2816]{2,1,0:T(8,128)(2,1)S(1)} %all_to_all.27.message, bf16[2,192,2304]{2,1,0:T(8,128)(2,1)S(1)} %copy-done, bf16[16,48,192]{2,1,0:T(8,128)(2,1)S(1)} %copy-done.5, s32[16,48,192]{2,1,0:T(8,128)S(1)} %copy-done.3), custom_call_target="tpu_custom_call" | custom-call | tf_op jit(solution)/shard_map/score/pallas_call | solution.py:207
  (1 shorter events, 0.0 us)
Async XLA Ops:
  0.0 47.1 %copy-start.8 = (s32[16]{0:T(128)S(1)}, s32[16]{0:T(128)}, u32[]{:S(2)}) copy-start(s32[16]{0:T(128)} %position.3) | copy-start | bytes 196
  0.0 47.1 %copy-start.7 = (f32[16,48]{1,0:T(8,128)S(1)}, f32[16,48]{1,0:T(8,128)}, u32[]{:S(2)}) copy-start(f32[16,48]{1,0:T(8,128)} %inv_rms.1) | copy-start | bytes 9220
  0.0 1.3 %copy-start.1 = (bf16[250,2304]{1,0:T(8,128)(2,1)S(1)}, bf16[250,2304]{1,0:T(8,128)(2,1)}, u32[]{:S(2)}) copy-start(bf16[250,2304]{1,0:T(8,128)(2,1)} %unembed.1) | copy-start | bytes 3456004
  1.3 0.7 copy-start.9
  2.0 45.1 %copy-start.2 = (bf16[1,256,2304]{2,1,0:T(8,128)(2,1)S(1)}, bf16[1,256,2304]{2,1,0:T(8,128)(2,1)}, u32[]{:S(2)}) copy-start(bf16[1,256,2304]{2,1,0:T(8,128)(2,1)} %param.18) | copy-start | bytes 3538948
  2.0 45.1 %copy-start.6 = (f32[1,16,48,48]{3,2,1,0:T(8,128)S(1)}, f32[1,16,48,48]{3,2,1,0:T(8,128)}, u32[]{:S(2)}) copy-start(f32[1,16,48,48]{3,2,1,0:T(8,128)} %param.14) | copy-start | bytes 442372
  20.8 39.0 %copy-start.4 = (bf16[4,288,256]{2,1,0:T(8,128)(2,1)S(1)}, bf16[4,288,256]{2,1,0:T(8,128)(2,1)}, u32[]{:S(2)}) copy-start(bf16[4,288,256]{2,1,0:T(8,128)(2,1)} %w_value.1) | copy-start | bytes 1769476
  21.4 25.6 %all-to-all-start.1 = ((bf16[16,18,128]{2,1,0:T(8,128)(2,1)}), bf16[16,18,128]{2,1,0:T(8,128)(2,1)S(1)}, u32[]{:S(2)}, u32[]{:S(2)}) async-start(bf16[16,18,128]{2,1,0:T(8,128)(2,1)} %sum_and_repeat.1), calls=%async_computation.1 | async-start | bytes 196608 | tf_op jit(solution)/shard_map/all_to_all | solution.py:190
  48.7 11.0 %all-to-all-start.2 = ((f32[8,8,128]{2,1,0:T(8,128)}), f32[8,8,128]{2,1,0:T(8,128)S(1)}, u32[]{:S(2)}, u32[]{:S(2)}) async-start(f32[8,8,128]{2,1,0:T(8,128)} %get-tuple-element.7), calls=%async_computation.2 | async-start | bytes 65536 | tf_op jit(solution)/shard_map/all_to_all | solution.py:197
  59.7 23.4 %copy-start.3 = (s32[16,48,192]{2,1,0:T(8,128)S(1)}, s32[16,48,192]{2,1,0:T(8,128)}, u32[]{:S(2)}) copy-start(s32[16,48,192]{2,1,0:T(8,128)} %active.1) | copy-start | bytes 1769476
  60.0 23.2 %copy-start = (bf16[2,192,2304]{2,1,0:T(8,128)(2,1)S(1)}, bf16[2,192,2304]{2,1,0:T(8,128)(2,1)}, u32[]{:S(2)}) copy-start(bf16[2,192,2304]{2,1,0:T(8,128)(2,1)} %decoder.1) | copy-start | bytes 5308420
  60.0 23.2 %copy-start.5 = (bf16[16,48,192]{2,1,0:T(8,128)(2,1)S(1)}, bf16[16,48,192]{2,1,0:T(8,128)(2,1)}, u32[]{:S(2)}) copy-start(bf16[16,48,192]{2,1,0:T(8,128)(2,1)} %activation.1) | copy-start | bytes 884740

commit v4 on v3

--- a/solution.py
+++ b/solution.py
@@ -1,5 +1,3 @@
-import functools
-
 import jax
 import jax.numpy as jnp
 from jax import lax
@@ -16,6 +14,7 @@
 NT = (((1,), (1,)), ((), ()))
 VMEM = pl.BlockSpec(memory_space=pltpu.VMEM)
 SMEM = pl.BlockSpec(memory_space=pltpu.SMEM)
+HBM = pl.BlockSpec(memory_space=pltpu.HBM)
 
 
 def call(body, shapes, in_specs, name):
@@ -33,19 +32,25 @@
     return jax.ShapeDtypeStruct(dims, kind)
 
 
-def pick_rows(ids, first, unembed, out):
+def pick_rows(first, ids_hbm, unembed_hbm, out, ids, unembed, sems):
+    ids_copy = pltpu.make_async_copy(ids_hbm, ids, sems.at[0])
+    rows_copy = pltpu.make_async_copy(unembed_hbm, unembed, sems.at[1])
+    ids_copy.start()
+    rows_copy.start()
     targets = ids.shape[0]
     rows, width = unembed.shape
     index = lax.broadcasted_iota(jnp.int32, (targets, rows), 0)
     wanted = jnp.zeros((targets, rows), jnp.int32)
+    ids_copy.wait()
     for g in range(targets):
         wanted = jnp.where(index == g, ids[g] - first[0], wanted)
     picker = (wanted == lax.broadcasted_iota(jnp.int32, (targets, rows), 1)).astype(BF16)
+    rows_copy.wait()
     found = jnp.dot(picker, unembed[...], preferred_element_type=F32)
+    half = width // 2
     for g in range(targets):
-        row = jnp.concatenate(
-            [found[g : g + 1, k * LANES : (k + 1) * LANES] for k in range(width // LANES)], axis=0
-        ).astype(BF16)
+        row = jnp.concatenate([found[g : g + 1, :half], found[g : g + 1, half:]], axis=0)
+        row = row.astype(BF16)
         out[2 * g] = row
         out[2 * g + 1] = row
 
@@ -65,8 +70,8 @@
 
 def query_gradient(position, target, parts, w_out, attn, inv_rms, row_out, out):
     row = total(parts)
-    row_out[...] = row.astype(BF16)
-    flat = jnp.concatenate([row[k : k + 1, :] for k in range(row.shape[0])], axis=1).astype(BF16)
+    row_out[...] = row
+    flat = jnp.concatenate([row[0:1], row[1:2]], axis=1).astype(BF16)
     gradient = lax.dot_general(flat, w_out[...], NT, preferred_element_type=F32)
     here = position[target[0]]
     weights = attn[target[0], pl.ds(here, 1), :]
@@ -82,7 +87,7 @@
         out[i, 2:3, positions:] = jnp.zeros((1, LANES - positions), F32)
 
 
-def lower_block(heard, w_value, gain, out):
+def lower_block(block, heard, w_value, gain, out):
     heads = heard.shape[0]
     kv_heads, columns, _ = w_value.shape
     gradient = jnp.concatenate([heard[:, 0, :], heard[:, 1, :]], axis=1).astype(BF16)
@@ -91,7 +96,11 @@
     for v in range(kv_heads):
         value = lax.dot_general(gradient, w_value[v], NT, preferred_element_type=F32)
         lowered = jnp.where(head // (heads // kv_heads) == v, value, lowered)
-    lowered = (lowered * gain[...]).astype(BF16)
+    own_gain = jnp.zeros((1, columns), F32)
+    for i in range(heads):
+        part = gain[:, i * columns : (i + 1) * columns]
+        own_gain = jnp.where(block[0] == i, part, own_gain)
+    lowered = (lowered * own_gain).astype(BF16)
     for i in range(out.shape[0]):
         out[i] = lowered
 
@@ -106,16 +115,17 @@
     low = scale - high
     both = (high + pltpu.roll(low, LANES // 2, 1)).astype(BF16)
     lowered = lowered.astype(BF16)
-    rows = row[...].astype(F32)
-    count = rows.shape[0]
+    half = row.shape[1] // LANES
+    rows = [
+        row[k // half : k // half + 1, (k % half) * LANES : (k % half + 1) * LANES]
+        for k in range(2 * half)
+    ]
+    rows = rows + [jnp.zeros((1, LANES), F32)] * (-len(rows) % heads)
     for i in range(out.shape[0]):
         out[i, :, 0:width] = lowered
         out[i, :, width : width + LANES] = both
-    for j in range(-(-count // heads)):
-        some = rows[j * heads : min((j + 1) * heads, count)]
-        if some.shape[0] < heads:
-            some = jnp.concatenate([some, jnp.zeros((heads - some.shape[0], LANES), F32)], axis=0)
-        some = some.astype(BF16)
+    for j in range(len(rows) // heads):
+        some = jnp.concatenate(rows[j * heads : (j + 1) * heads], axis=0).astype(BF16)
         start = width + (j + 1) * LANES
         for i in range(out.shape[0]):
             out[i, :, start : start + LANES] = some
@@ -134,27 +144,39 @@
         ],
         axis=1,
     ).astype(BF16)
-    own = lax.dot_general(direction, decoder[0], NT, preferred_element_type=F32)
-    own = own + lax.dot_general(direction, decoder[1], NT, preferred_element_type=F32)
     lowered = message[:, :, 0:width].reshape(targets * heads, width)
-    per_head = lax.dot_general(lowered, decoder[0], NT, preferred_element_type=F32)
+    both = jnp.concatenate([lowered, direction], axis=0)
+    bottom = lax.dot_general(both, decoder[0], NT, preferred_element_type=F32)
+    top = lax.dot_general(direction, decoder[1], NT, preferred_element_type=F32)
+    per_head = bottom[0 : targets * heads]
+    own = bottom[targets * heads :] + top
+    per_head_high = per_head.astype(BF16).astype(F32)
+    per_head_low = per_head - per_head_high
+    own_high = own.astype(BF16).astype(F32)
+    own_low = own - own_high
     scale = message[:, :, width : width + LANES].astype(F32)
     key = lax.broadcasted_iota(jnp.int32, (heads, LANES), 1)
-    first = lax.broadcasted_iota(jnp.int32, (heads, LANES), 0) == 0
-    spare = jnp.zeros((heads - 1, features), F32)
+    below_two = lax.broadcasted_iota(jnp.int32, (heads, LANES), 0) < 2
+    spare = jnp.zeros((heads - 2, features), F32)
     for g in range(targets):
-        both = scale[g] + pltpu.roll(scale[g], LANES // 2, 1)
-        here = jnp.where(first & (key == position[g]), 1.0, 0.0)
-        left = jnp.concatenate([both, here], axis=0)[:, 0:positions]
+        high = scale[g]
+        low = pltpu.roll(high, LANES // 2, 1)
+        here = jnp.where(below_two & (key == position[g]), 1.0, 0.0)
+        mine = slice(g * heads, (g + 1) * heads)
+        left = jnp.concatenate([high, low, high, here], axis=0)[:, 0:positions].astype(BF16)
         right = jnp.concatenate(
-            [per_head[g * heads : (g + 1) * heads], own[g : g + 1], spare], axis=0
-        )
+            [
+                per_head_high[mine],
+                per_head_high[mine],
+                per_head_low[mine],
+                own_high[g : g + 1],
+                own_low[g : g + 1],
+                spare,
+            ],
+            axis=0,
+        ).astype(BF16)
         scores = lax.dot_general(
-            left,
-            right,
-            (((0,), (0,)), ((), ())),
-            precision=lax.Precision.HIGHEST,
-            preferred_element_type=F32,
+            left, right, (((0,), (0,)), ((), ())), preferred_element_type=F32
         )
         out[g] = activation[g].astype(F32) * active[g].astype(F32) * scores
 
@@ -179,25 +201,44 @@
     heads = lax.axis_size(MP)
     first_row = (lax.axis_index(ALL) * vocab_rows).reshape(1)
     target = lax.axis_index(("x", "y")).reshape(1)
-    gain = lax.dynamic_slice_in_dim(norm_gain, lax.axis_index(MP) * columns, columns, 0)[None]
-
-    found = call(
-        pick_rows, shape((2 * targets, tiles, LANES), BF16), [SMEM, SMEM, VMEM], "pick_rows"
-    )(target_ids, first_row, unembed)
+    block = lax.axis_index(MP).reshape(1)
+
+    found = pl.pallas_call(
+        pick_rows,
+        out_shape=shape((2 * targets, 2, width // 2), BF16),
+        in_specs=[SMEM, HBM, HBM],
+        out_specs=VMEM,
+        scratch_shapes=[
+            pltpu.SMEM((targets,), jnp.int32),
+            pltpu.VMEM((vocab_rows, width), BF16),
+            pltpu.SemaphoreType.DMA((2,)),
+        ],
+        name="pick_rows",
+        compiler_params=pltpu.CompilerParams(vmem_limit_bytes=32 * 1024 * 1024),
+    )(
+        first_row,
+        pltpu.with_memory_space_constraint(target_ids, pltpu.HBM),
+        pltpu.with_memory_space_constraint(unembed, pltpu.HBM),
+    )
     parts = lax.all_to_all(found, ("x", "y", "core"), 0, 0, tiled=True)
     ring = lax.axis_size(("zl", "zh"))
-    parts = call(sum_and_repeat, shape((ring, tiles, LANES), BF16), [VMEM], "sum_and_repeat")(parts)
+    parts = call(
+        sum_and_repeat, shape((ring, 2, width // 2), BF16), [VMEM], "sum_and_repeat"
+    )(parts)
     parts = lax.all_to_all(parts, ("zl", "zh"), 0, 0, tiled=True)
     row, asked = call(
         query_gradient,
-        (shape((tiles, LANES), BF16), shape((heads, 8, LANES), F32)),
+        (shape((2, width // 2), F32), shape((heads, 8, LANES), F32)),
         [SMEM, SMEM, VMEM, VMEM, VMEM, VMEM],
         "query_gradient",
     )(target_pos, target, parts, w_out[0], attn_weights[0], inv_rms)
     heard = lax.all_to_all(asked, MP, 0, 0, tiled=True)
     blocks = call(
-        lower_block, shape((heads, heads, columns), BF16), [VMEM, VMEM, VMEM], "lower_block"
-    )(heard, w_value, gain)
+        lower_block,
+        shape((heads, heads, columns), BF16),
+        [SMEM, VMEM, VMEM, VMEM],
+        "lower_block",
+    )(block, heard, w_value, norm_gain[None])
     blocks = lax.all_to_all(blocks, MP, 0, 0, tiled=True)
     length = width + LANES + -(-tiles // heads) * LANES
     message = call(

time: 87 us -> 84.2 us (0.968)
  local copies, waits for them, and re-layouts: 2.76 us -> 0.07 us
    unnamed x20 -> x18, local copies, waits for them, and re-layouts: 1.98 us -> 0.06 us
    pallas_call x4, Pallas kernels: 3.39 us -> 4.57 us  [the longest x1 1.73 us: on_device(): pl.pallas_call(pick_rows, out_shape=shape((2 * targets, 2, width // 2), B...]
    pallas_call x1, Pallas kernels: 3.44 us -> 2.47 us  [on_device(): call(score, shape(activation.shape, F32), [SMEM, VMEM, VMEM, VMEM, VMEM],...]
  transfers between devices with their start and end apart: 2 -> 2, of which waited for: 2 -> 2; matrix products, arithmetic and copies ran while one was open for 1% -> 0% of each run, Pallas kernels for 0% -> 0%
where the time goes in v4:
time: 84.2 us; the launch traced here: 83.8 us
  blocking collectives  40.7 us (48%)
  starting transfers between devices  19.1 us (23%)
  waiting for transfers between devices  16.7 us (20%)
  Pallas kernels  7.16 us (9%)
    all_to_all x1, blocking collectives, on_device(): parts = lax.all_to_all(found, ('x', 'y', 'core'), 0, 0, tiled=True)  17.6 us
    all_to_all x1, blocking collectives, on_device(): message = lax.all_to_all(message, ('x', 'y'), 0, 0, tiled=True)  14.8 us
    all_to_all x1, starting transfers between devices, on_device(): parts = lax.all_to_all(parts, ('zl', 'zh'), 0, 0, tiled=True)  13.7 us
    all_to_all x1, waiting for transfers between devices, on_device(): parts = lax.all_to_all(parts, ('zl', 'zh'), 0, 0, tiled=True)  11.7 us
    all_to_all x1, blocking collectives, on_device(): blocks = lax.all_to_all(blocks, MP, 0, 0, tiled=True)  8.29 us
    all_to_all x1, starting transfers between devices, on_device(): heard = lax.all_to_all(asked, MP, 0, 0, tiled=True)  5.34 us
    all_to_all x1, waiting for transfers between devices, on_device(): heard = lax.all_to_all(asked, MP, 0, 0, tiled=True)  4.99 us
    pallas_call x1, Pallas kernels, on_device(): call(score, shape(activation.shape, F32), [SMEM, VMEM, VMEM, VMEM, VMEM],...  2.47 us
  transfers between devices with their start and end apart: 2, of which 2 were waited for; matrix products, arithmetic and copies ran while one was open for 0% of the time, Pallas kernels for 0%

profile of v4, /device:TPU:1, one launch (start us, length us, event | category | flops | bytes accessed | tf_op | source)
XLA Modules:
  0.0 83.8 jit_solution(14742542961681899657)
XLA Ops:
  0.0 0.0 copy-start.7
  0.0 0.0 copy-start.1
  0.0 0.0 copy-start.6
  0.0 0.0 copy-start.5
  0.0 1.7 %pick_rows.1 = bf16[32,2,1152]{2,1,0:T(2,128)(2,1)S(1)} custom-call(s32[1]{0:T(128)} %bitcast.2.first, s32[16]{0:T(128)} %ids_hbm.1, bf16[250,2304]{1,0:T(8,128)(2,1)} %unembed_hbm.1), custom_call_target="tpu_custom_call" | custom-call | tf_op jit(solution)/shard_map/pick_rows/pallas_call | solution.py:206
  1.8 0.0 copy-start.8
  1.8 0.0 copy-start.3
  1.8 17.6 %all_to_all.25.parts = bf16[32,2,1152]{2,1,0:T(2,128)(2,1)S(1)} all-to-all(bf16[32,2,1152]{2,1,0:T(2,128)(2,1)S(1)} %pick_rows.1), channel_id=1, replica_groups=mesh['zl'=4,'core'=2,'x'=4,'zh'=4,'y'=4] {'x','y','core'}, dimensions={0} | all-to-all | bytes 294912 | tf_op jit(solution)/shard_map/all_to_all | solution.py:223
  19.4 0.7 sum_and_repeat.1
  20.0 13.7 %all-to-all-start.1 = ((bf16[16,2,1152]{2,1,0:T(2,128)(2,1)}), bf16[16,2,1152]{2,1,0:T(2,128)(2,1)S(1)}, u32[]{:S(2)}, u32[]{:S(2)}) async-start(bf16[16,2,1152]{2,1,0:T(2,128)(2,1)} %sum_and_repeat.1), calls=%async_computation.1 | async-start | bytes 147456 | tf_op jit(solution)/shard_map/all_to_all | solution.py:228
  33.8 11.7 %all-to-all-done.1.parts = bf16[16,2,1152]{2,1,0:T(2,128)(2,1)S(1)} async-done(((bf16[16,2,1152]{2,1,0:T(2,128)(2,1)}), bf16[16,2,1152]{2,1,0:T(2,128)(2,1)S(1)}, u32[]{:S(2)}, u32[]{:S(2)}) %all-to-all-start.1) | async-done | bytes 73760 | tf_op jit(solution)/shard_map/all_to_all | solution.py:228
  45.5 0.0 copy-done.7
  45.5 0.0 copy-done.1
  45.5 0.0 copy-done.6
  45.5 0.0 copy-done.5
  45.5 1.6 %query_gradient.1 = (f32[2,1152]{1,0:T(2,128)S(1)}, f32[8,8,128]{2,1,0:T(8,128)}) custom-call(s32[16]{0:T(128)S(1)} %copy-done.7, s32[1]{0:T(128)} %bitcast.1.target, bf16[16,2,1152]{2,1,0:T(2,128)(2,1)S(1)} %all-to-all-done.1.parts, bf16[256,2304]{1,0:T(8,128)(2,1)S(1)} %bitcast.5, f32[16,48,48]{2,1,0:T(8,128)S(1)} %bitcast.6, f32[16,48]{1,0:T(8,128)S(1)} %copy-done.6), custom_call_target="tpu_custom_call" | custom-call | tf_op jit(solution)/shard_map/query_gradient/pallas_call | solution.py:229
  47.2 5.3 %all-to-all-start.2 = ((f32[8,8,128]{2,1,0:T(8,128)}), f32[8,8,128]{2,1,0:T(8,128)S(1)}, u32[]{:S(2)}, u32[]{:S(2)}) async-start(f32[8,8,128]{2,1,0:T(8,128)} %get-tuple-element.7), calls=%async_computation.2 | async-start | bytes 65536 | tf_op jit(solution)/shard_map/all_to_all | solution.py:235
  52.5 0.0 copy-done.8
  52.5 5.0 %all-to-all-done.2.heard = f32[8,8,128]{2,1,0:T(8,128)S(1)} async-done(((f32[8,8,128]{2,1,0:T(8,128)}), f32[8,8,128]{2,1,0:T(8,128)S(1)}, u32[]{:S(2)}, u32[]{:S(2)}) %all-to-all-start.2) | async-done | bytes 32800 | tf_op jit(solution)/shard_map/all_to_all | solution.py:235
  57.5 0.0 copy-done.3
  57.5 0.0 copy-start.2
  57.5 0.5 lower_block.1
  58.0 0.0 copy-start
  58.1 0.0 copy-start.4
  58.1 8.3 %all_to_all.26.blocks = bf16[8,8,288]{2,1,0:T(8,128)(2,1)S(1)} all-to-all(bf16[8,8,288]{2,1,0:T(8,128)(2,1)S(1)} %lower_block.1), channel_id=1, replica_groups=mesh['zl'=4,'core'=2,'x'=4,'zh'=4,'y'=4] {'zl','core'}, dimensions={0} | all-to-all | bytes 73728 | tf_op jit(solution)/shard_map/all_to_all | solution.py:242
  66.4 0.1 build_message.1
  66.5 14.8 %all_to_all.27.message = bf16[16,8,2816]{2,1,0:T(8,128)(2,1)S(1)} all-to-all(bf16[16,8,2816]{2,1,0:T(8,128)(2,1)S(1)} %build_message.1), channel_id=1, replica_groups=mesh['zl'=4,'core'=2,'x'=4,'zh'=4,'y'=4] {'x','y'}, dimensions={0} | all-to-all | bytes 1441792 | tf_op jit(solution)/shard_map/all_to_all | solution.py:247
  81.3 0.0 copy-done.2
  81.4 0.0 copy-done
  81.4 0.0 copy-done.4
  81.4 2.5 %score.1 = f32[16,48,192]{2,1,0:T(8,128)} custom-call(s32[16]{0:T(128)S(1)} %copy-done.7, bf16[16,8,2816]{2,1,0:T(8,128)(2,1)S(1)} %all_to_all.27.message, bf16[2,192,2304]{2,1,0:T(8,128)(2,1)S(1)} %copy-done, bf16[16,48,192]{2,1,0:T(8,128)(2,1)S(1)} %copy-done.4, s32[16,48,192]{2,1,0:T(8,128)S(1)} %copy-done.2), custom_call_target="tpu_custom_call" | custom-call | tf_op jit(solution)/shard_map/score/pallas_call | solution.py:248
  (1 shorter events, 0.0 us)
Async XLA Ops:
  0.0 45.5 %copy-start.7 = (s32[16]{0:T(128)S(1)}, s32[16]{0:T(128)}, u32[]{:S(2)}) copy-start(s32[16]{0:T(128)} %position.3) | copy-start | bytes 196
  0.0 45.5 %copy-start.1 = (bf16[1,256,2304]{2,1,0:T(8,128)(2,1)S(1)}, bf16[1,256,2304]{2,1,0:T(8,128)(2,1)}, u32[]{:S(2)}) copy-start(bf16[1,256,2304]{2,1,0:T(8,128)(2,1)} %param.18) | copy-start | bytes 3538948
  0.0 45.5 %copy-start.6 = (f32[16,48]{1,0:T(8,128)S(1)}, f32[16,48]{1,0:T(8,128)}, u32[]{:S(2)}) copy-start(f32[16,48]{1,0:T(8,128)} %inv_rms.1) | copy-start | bytes 9220
  0.0 45.5 %copy-start.5 = (f32[1,16,48,48]{3,2,1,0:T(8,128)S(1)}, f32[1,16,48,48]{3,2,1,0:T(8,128)}, u32[]{:S(2)}) copy-start(f32[1,16,48,48]{3,2,1,0:T(8,128)} %param.14) | copy-start | bytes 442372
  1.8 50.7 %copy-start.8 = (f32[2304]{0:T(1024)S(1)}, f32[2304]{0:T(1024)}, u32[]{:S(2)}) copy-start(f32[2304]{0:T(1024)} %param.16) | copy-start | bytes 27652
  1.8 55.7 %copy-start.3 = (bf16[4,288,256]{2,1,0:T(8,128)(2,1)S(1)}, bf16[4,288,256]{2,1,0:T(8,128)(2,1)}, u32[]{:S(2)}) copy-start(bf16[4,288,256]{2,1,0:T(8,128)(2,1)} %w_value.1) | copy-start | bytes 1769476
  20.0 25.5 %all-to-all-start.1 = ((bf16[16,2,1152]{2,1,0:T(2,128)(2,1)}), bf16[16,2,1152]{2,1,0:T(2,128)(2,1)S(1)}, u32[]{:S(2)}, u32[]{:S(2)}) async-start(bf16[16,2,1152]{2,1,0:T(2,128)(2,1)} %sum_and_repeat.1), calls=%async_computation.1 | async-start | bytes 147456 | tf_op jit(solution)/shard_map/all_to_all | solution.py:228
  47.2 10.3 %all-to-all-start.2 = ((f32[8,8,128]{2,1,0:T(8,128)}), f32[8,8,128]{2,1,0:T(8,128)S(1)}, u32[]{:S(2)}, u32[]{:S(2)}) async-start(f32[8,8,128]{2,1,0:T(8,128)} %get-tuple-element.7), calls=%async_computation.2 | async-start | bytes 65536 | tf_op jit(solution)/shard_map/all_to_all | solution.py:235
  57.5 23.9 %copy-start.2 = (s32[16,48,192]{2,1,0:T(8,128)S(1)}, s32[16,48,192]{2,1,0:T(8,128)}, u32[]{:S(2)}) copy-start(s32[16,48,192]{2,1,0:T(8,128)} %active.1) | copy-start | bytes 1769476
  58.0 23.3 %copy-start = (bf16[2,192,2304]{2,1,0:T(8,128)(2,1)S(1)}, bf16[2,192,2304]{2,1,0:T(8,128)(2,1)}, u32[]{:S(2)}) copy-start(bf16[2,192,2304]{2,1,0:T(8,128)(2,1)} %decoder.1) | copy-start | bytes 5308420
  58.1 23.3 %copy-start.4 = (bf16[16,48,192]{2,1,0:T(8,128)(2,1)S(1)}, bf16[16,48,192]{2,1,0:T(8,128)(2,1)}, u32[]{:S(2)}) copy-start(bf16[16,48,192]{2,1,0:T(8,128)(2,1)} %activation.1) | copy-start | bytes 884740

commit v5 on v4

--- a/solution.py
+++ b/solution.py
@@ -32,23 +32,10 @@
     return jax.ShapeDtypeStruct(dims, kind)
 
 
-def pick_rows(first, ids_hbm, unembed_hbm, out, ids, unembed, sems):
-    ids_copy = pltpu.make_async_copy(ids_hbm, ids, sems.at[0])
-    rows_copy = pltpu.make_async_copy(unembed_hbm, unembed, sems.at[1])
-    ids_copy.start()
-    rows_copy.start()
-    targets = ids.shape[0]
-    rows, width = unembed.shape
-    index = lax.broadcasted_iota(jnp.int32, (targets, rows), 0)
-    wanted = jnp.zeros((targets, rows), jnp.int32)
-    ids_copy.wait()
-    for g in range(targets):
-        wanted = jnp.where(index == g, ids[g] - first[0], wanted)
-    picker = (wanted == lax.broadcasted_iota(jnp.int32, (targets, rows), 1)).astype(BF16)
-    rows_copy.wait()
-    found = jnp.dot(picker, unembed[...], preferred_element_type=F32)
-    half = width // 2
-    for g in range(targets):
+def share_rows(target, block, found, out):
+    del target, block
+    half = out.shape[2]
+    for g in range(found.shape[0]):
         row = jnp.concatenate([found[g : g + 1, :half], found[g : g + 1, half:]], axis=0)
         row = row.astype(BF16)
         out[2 * g] = row
@@ -96,9 +83,10 @@
     for v in range(kv_heads):
         value = lax.dot_general(gradient, w_value[v], NT, preferred_element_type=F32)
         lowered = jnp.where(head // (heads // kv_heads) == v, value, lowered)
+    whole = gain[...].reshape(1, heads * columns)
     own_gain = jnp.zeros((1, columns), F32)
     for i in range(heads):
-        part = gain[:, i * columns : (i + 1) * columns]
+        part = whole[:, i * columns : (i + 1) * columns]
         own_gain = jnp.where(block[0] == i, part, own_gain)
     lowered = (lowered * own_gain).astype(BF16)
     for i in range(out.shape[0]):
@@ -131,7 +119,7 @@
             out[i, :, start : start + LANES] = some
 
 
-def score(position, message, decoder, activation, active, out):
+def score(position, message, decoder, activation, active, out_hbm, out, sems):
     targets, heads, _ = message.shape
     _, features, width = decoder.shape
     positions = activation.shape[1]
@@ -158,6 +146,8 @@
     key = lax.broadcasted_iota(jnp.int32, (heads, LANES), 1)
     below_two = lax.broadcasted_iota(jnp.int32, (heads, LANES), 0) < 2
     spare = jnp.zeros((heads - 2, features), F32)
+    step = targets // 4
+    copies = []
     for g in range(targets):
         high = scale[g]
         low = pltpu.roll(high, LANES // 2, 1)
@@ -179,6 +169,15 @@
             left, right, (((0,), (0,)), ((), ())), preferred_element_type=F32
         )
         out[g] = activation[g].astype(F32) * active[g].astype(F32) * scores
+        if (g + 1) % step == 0:
+            copies.append(
+                pltpu.make_async_copy(
+                    out.at[g + 1 - step : g + 1], out_hbm.at[g + 1 - step : g + 1], sems.at[g // step]
+                )
+            )
+            copies[-1].start()
+    for copy in copies:
+        copy.wait()
 
 
 def on_device(
@@ -199,27 +198,16 @@
     tiles = width // LANES
     columns = w_value.shape[1]
     heads = lax.axis_size(MP)
-    first_row = (lax.axis_index(ALL) * vocab_rows).reshape(1)
+    first_row = lax.axis_index(ALL) * vocab_rows
     target = lax.axis_index(("x", "y")).reshape(1)
     block = lax.axis_index(MP).reshape(1)
 
-    found = pl.pallas_call(
-        pick_rows,
-        out_shape=shape((2 * targets, 2, width // 2), BF16),
-        in_specs=[SMEM, HBM, HBM],
-        out_specs=VMEM,
-        scratch_shapes=[
-            pltpu.SMEM((targets,), jnp.int32),
-            pltpu.VMEM((vocab_rows, width), BF16),
-            pltpu.SemaphoreType.DMA((2,)),
-        ],
-        name="pick_rows",
-        compiler_params=pltpu.CompilerParams(vmem_limit_bytes=32 * 1024 * 1024),
-    )(
-        first_row,
-        pltpu.with_memory_space_constraint(target_ids, pltpu.HBM),
-        pltpu.with_memory_space_constraint(unembed, pltpu.HBM),
-    )
+    own = first_row + jnp.arange(vocab_rows, dtype=jnp.int32)
+    picker = (target_ids[:, None] == own[None, :]).astype(BF16)
+    found = jnp.dot(picker, unembed, preferred_element_type=F32)
+    found = call(
+        share_rows, shape((2 * targets, 2, width // 2), BF16), [SMEM, SMEM, VMEM], "share_rows"
+    )(target, block, found)
     parts = lax.all_to_all(found, ("x", "y", "core"), 0, 0, tiled=True)
     ring = lax.axis_size(("zl", "zh"))
     parts = call(
@@ -238,16 +226,22 @@
         shape((heads, heads, columns), BF16),
         [SMEM, VMEM, VMEM, VMEM],
         "lower_block",
-    )(block, heard, w_value, norm_gain[None])
+    )(block, heard, w_value, norm_gain)
     blocks = lax.all_to_all(blocks, MP, 0, 0, tiled=True)
     length = width + LANES + -(-tiles // heads) * LANES
     message = call(
         build_message, shape((targets, heads, length), BF16), [VMEM, VMEM, VMEM], "build_message"
     )(blocks, heard, row)
     message = lax.all_to_all(message, ("x", "y"), 0, 0, tiled=True)
-    return call(score, shape(activation.shape, F32), [SMEM, VMEM, VMEM, VMEM, VMEM], "score")(
-        target_pos, message, decoder, activation, active
-    )
+    return pl.pallas_call(
+        score,
+        out_shape=shape(activation.shape, F32),
+        in_specs=[SMEM, VMEM, VMEM, VMEM, VMEM],
+        out_specs=HBM,
+        scratch_shapes=[pltpu.VMEM(activation.shape, F32), pltpu.SemaphoreType.DMA((4,))],
+        name="score",
+        compiler_params=pltpu.CompilerParams(vmem_limit_bytes=32 * 1024 * 1024),
+    )(target_pos, message, decoder, activation, active)
 
 
 def solution(mesh):

time: 84.2 us -> 82.3 us (0.977)
  blocking collectives: 40.7 us -> 75.8 us
  starting transfers between devices: 19.1 us -> 0 us
  waiting for transfers between devices: 16.7 us -> 0 us
  Pallas kernels: 7.16 us -> 3.82 us
  local copies, waits for them, and re-layouts: 0.07 us -> 1.26 us
  matrix products: 0 us -> 0.96 us
    all_to_all x0 -> x2, blocking collectives: none -> 35.2 us  [the longest x1 25.2 us: on_device(): parts = lax.all_to_all(parts, ('zl', 'zh'), 0, 0, tiled=True)]
    all_to_all x2 -> x0, starting transfers between devices: 19.1 us -> none  [the longest x1 13.7 us: on_device(): parts = lax.all_to_all(parts, ('zl', 'zh'), 0, 0, tiled=True)]
    all_to_all x2 -> x0, waiting for transfers between devices: 16.7 us -> none  [the longest x1 11.7 us: on_device(): parts = lax.all_to_all(parts, ('zl', 'zh'), 0, 0, tiled=True)]
    pallas_call x2, Pallas kernels: 4.2 us -> 2.46 us  [the longest x1 2.35 us: on_device(): pl.pallas_call(score, out_shape=shape(activation.shape, F32), in_specs=[S...]
    unnamed x18 -> x20, local copies, waits for them, and re-layouts: 0.06 us -> 1.26 us
    dot_general x0 -> x1, matrix products: none -> 0.96 us  [on_device(): found = jnp.dot(picker, unembed, preferred_element_type=F32)]
  transfers between devices with their start and end apart: 2 -> 0, of which waited for: 2 -> 0; matrix products, arithmetic and copies ran while one was open for 0% -> 0% of each run, Pallas kernels for 0% -> 0%
where the time goes in v5:
time: 82.3 us; the launch traced here: 82 us
  blocking collectives  75.8 us (92%)
  Pallas kernels  3.82 us (5%)
  local copies, waits for them, and re-layouts  1.26 us (2%)
  matrix products  0.96 us (1%)
    all_to_all x1, blocking collectives, on_device(): parts = lax.all_to_all(parts, ('zl', 'zh'), 0, 0, tiled=True)  25.2 us
    all_to_all x1, blocking collectives, on_device(): parts = lax.all_to_all(found, ('x', 'y', 'core'), 0, 0, tiled=True)  17.6 us
    all_to_all x1, blocking collectives, on_device(): message = lax.all_to_all(message, ('x', 'y'), 0, 0, tiled=True)  14.7 us
    all_to_all x1, blocking collectives, on_device(): heard = lax.all_to_all(asked, MP, 0, 0, tiled=True)  9.99 us
    all_to_all x1, blocking collectives, on_device(): blocks = lax.all_to_all(blocks, MP, 0, 0, tiled=True)  8.29 us
    pallas_call x1, Pallas kernels, on_device(): pl.pallas_call(score, out_shape=shape(activation.shape, F32), in_specs=[S...  2.35 us

profile of v5, /device:TPU:1, one launch (start us, length us, event | category | flops | bytes accessed | tf_op | source)
XLA Modules:
  0.0 82.0 jit_solution(1913617343689053950)
XLA Ops:
  0.0 0.0 copy-start
  0.0 0.0 copy-start.9
  0.0 0.0 copy-start.2
  0.0 0.0 copy-start.8
  0.0 0.0 copy-start.6
  0.1 1.2 %copy-done = bf16[250,2304]{1,0:T(8,128)(2,1)S(1)} copy-done((bf16[250,2304]{1,0:T(8,128)(2,1)S(1)}, bf16[250,2304]{1,0:T(8,128)(2,1)}, u32[]{:S(2)}) %copy-start) | copy-done | bytes 1152024
  1.3 1.0 %fusion.found = f32[16,2304]{1,0:T(8,128)S(1)} fusion(bf16[250,2304]{1,0:T(8,128)(2,1)S(1)} %copy-done, s32[250]{0:T(256)S(1)} %iota_add_fusion, s32[16]{0:T(128)} %param.11), kind=kOutput, calls=%fused_computation | convolution fusion | flops 18436000 | bytes 1300520 | tf_op jit(solution)/shard_map/dot_general | solution.py:207
  2.2 0.1 share_rows.1
  2.4 0.0 copy-start.4
  2.4 0.0 copy-start.7
  2.4 17.6 %all_to_all.25.parts = bf16[32,2,1152]{2,1,0:T(2,128)(2,1)S(1)} all-to-all(bf16[32,2,1152]{2,1,0:T(2,128)(2,1)S(1)} %share_rows.1), channel_id=1, replica_groups=mesh['zl'=4,'core'=2,'x'=4,'zh'=4,'y'=4] {'x','y','core'}, dimensions={0} | all-to-all | bytes 294912 | tf_op jit(solution)/shard_map/all_to_all | solution.py:211
  20.0 0.1 sum_and_repeat.1
  20.0 25.2 %all_to_all.26.parts = bf16[16,2,1152]{2,1,0:T(2,128)(2,1)S(1)} all-to-all(bf16[16,2,1152]{2,1,0:T(2,128)(2,1)S(1)} %sum_and_repeat.1), channel_id=1, replica_groups=mesh['zl'=4,'core'=2,'x'=4,'zh'=4,'y'=4] {'zl','zh'}, dimensions={0} | all-to-all | bytes 147456 | tf_op jit(solution)/shard_map/all_to_all | solution.py:216
  45.3 0.0 copy-done.9
  45.3 0.0 copy-done.2
  45.3 0.0 copy-done.8
  45.3 0.0 copy-done.6
  45.3 0.9 %query_gradient.1 = (f32[2,1152]{1,0:T(2,128)S(1)}, f32[8,8,128]{2,1,0:T(8,128)S(1)}) custom-call(s32[16]{0:T(128)S(1)} %copy-done.9, s32[1]{0:T(128)} %bitcast.1.target, bf16[16,2,1152]{2,1,0:T(2,128)(2,1)S(1)} %all_to_all.26.parts, bf16[256,2304]{1,0:T(8,128)(2,1)S(1)} %bitcast.5, f32[16,48,48]{2,1,0:T(8,128)S(1)} %bitcast.6, f32[16,48]{1,0:T(8,128)S(1)} %copy-done.8), custom_call_target="tpu_custom_call" | custom-call | tf_op jit(solution)/shard_map/query_gradient/pallas_call | solution.py:217
  46.2 10.0 %all_to_all.27.heard = f32[8,8,128]{2,1,0:T(8,128)S(1)} all-to-all(f32[8,8,128]{2,1,0:T(8,128)S(1)} %get-tuple-element.7), channel_id=1, replica_groups=mesh['zl'=4,'core'=2,'x'=4,'zh'=4,'y'=4] {'zl','core'}, dimensions={0} | all-to-all | bytes 65536 | tf_op jit(solution)/shard_map/all_to_all | solution.py:223
  56.2 0.0 copy-done.4
  56.2 0.0 copy-done.7
  56.2 0.0 copy-start.3
  56.2 0.3 lower_block.1
  56.5 0.0 copy-start.1
  56.5 0.0 copy-start.5
  56.5 8.3 %all_to_all.28.blocks = bf16[8,8,288]{2,1,0:T(8,128)(2,1)S(1)} all-to-all(bf16[8,8,288]{2,1,0:T(8,128)(2,1)S(1)} %lower_block.1), channel_id=1, replica_groups=mesh['zl'=4,'core'=2,'x'=4,'zh'=4,'y'=4] {'zl','core'}, dimensions={0} | all-to-all | bytes 73728 | tf_op jit(solution)/shard_map/all_to_all | solution.py:230
  64.8 0.1 build_message.1
  64.9 14.7 %all_to_all.29.message = bf16[16,8,2816]{2,1,0:T(8,128)(2,1)S(1)} all-to-all(bf16[16,8,2816]{2,1,0:T(8,128)(2,1)S(1)} %build_message.1), channel_id=1, replica_groups=mesh['zl'=4,'core'=2,'x'=4,'zh'=4,'y'=4] {'x','y'}, dimensions={0} | all-to-all | bytes 1441792 | tf_op jit(solution)/shard_map/all_to_all | solution.py:235
  79.6 0.0 copy-done.3
  79.6 0.0 copy-done.1
  79.6 0.0 copy-done.5
  79.6 2.3 %score.1 = f32[16,48,192]{2,1,0:T(8,128)} custom-call(s32[16]{0:T(128)S(1)} %copy-done.9, bf16[16,8,2816]{2,1,0:T(8,128)(2,1)S(1)} %all_to_all.29.message, bf16[2,192,2304]{2,1,0:T(8,128)(2,1)S(1)} %copy-done.1, bf16[16,48,192]{2,1,0:T(8,128)(2,1)S(1)} %copy-done.5, s32[16,48,192]{2,1,0:T(8,128)S(1)} %copy-done.3), custom_call_target="tpu_custom_call" | custom-call | tf_op jit(solution)/shard_map/score/pallas_call | solution.py:236
  (1 shorter events, 0.0 us)
Async XLA Ops:
  0.0 1.3 %copy-start = (bf16[250,2304]{1,0:T(8,128)(2,1)S(1)}, bf16[250,2304]{1,0:T(8,128)(2,1)}, u32[]{:S(2)}) copy-start(bf16[250,2304]{1,0:T(8,128)(2,1)} %param.13) | copy-start | bytes 3456004
  0.0 45.3 %copy-start.9 = (s32[16]{0:T(128)S(1)}, s32[16]{0:T(128)}, u32[]{:S(2)}) copy-start(s32[16]{0:T(128)} %position.3) | copy-start | bytes 196
  0.0 45.3 %copy-start.2 = (bf16[1,256,2304]{2,1,0:T(8,128)(2,1)S(1)}, bf16[1,256,2304]{2,1,0:T(8,128)(2,1)}, u32[]{:S(2)}) copy-start(bf16[1,256,2304]{2,1,0:T(8,128)(2,1)} %param.18) | copy-start | bytes 3538948
  0.0 45.3 %copy-start.8 = (f32[16,48]{1,0:T(8,128)S(1)}, f32[16,48]{1,0:T(8,128)}, u32[]{:S(2)}) copy-start(f32[16,48]{1,0:T(8,128)} %inv_rms.1) | copy-start | bytes 9220
  0.0 45.3 %copy-start.6 = (f32[1,16,48,48]{3,2,1,0:T(8,128)S(1)}, f32[1,16,48,48]{3,2,1,0:T(8,128)}, u32[]{:S(2)}) copy-start(f32[1,16,48,48]{3,2,1,0:T(8,128)} %param.14) | copy-start | bytes 442372
  2.4 53.9 %copy-start.4 = (bf16[4,288,256]{2,1,0:T(8,128)(2,1)S(1)}, bf16[4,288,256]{2,1,0:T(8,128)(2,1)}, u32[]{:S(2)}) copy-start(bf16[4,288,256]{2,1,0:T(8,128)(2,1)} %w_value.1) | copy-start | bytes 1769476
  2.4 53.8 %copy-start.7 = (f32[2304]{0:T(1024)S(1)}, f32[2304]{0:T(1024)}, u32[]{:S(2)}) copy-start(f32[2304]{0:T(1024)} %gain.1) | copy-start | bytes 27652
  56.2 23.4 %copy-start.3 = (s32[16,48,192]{2,1,0:T(8,128)S(1)}, s32[16,48,192]{2,1,0:T(8,128)}, u32[]{:S(2)}) copy-start(s32[16,48,192]{2,1,0:T(8,128)} %active.1) | copy-start | bytes 1769476
  56.5 23.2 %copy-start.1 = (bf16[2,192,2304]{2,1,0:T(8,128)(2,1)S(1)}, bf16[2,192,2304]{2,1,0:T(8,128)(2,1)}, u32[]{:S(2)}) copy-start(bf16[2,192,2304]{2,1,0:T(8,128)(2,1)} %decoder.1) | copy-start | bytes 5308420
  56.5 23.1 %copy-start.5 = (bf16[16,48,192]{2,1,0:T(8,128)(2,1)S(1)}, bf16[16,48,192]{2,1,0:T(8,128)(2,1)}, u32[]{:S(2)}) copy-start(bf16[16,48,192]{2,1,0:T(8,128)(2,1)} %activation.1) | copy-start | bytes 884740

commit v6 on v5

--- a/solution.py
+++ b/solution.py
@@ -9,6 +9,7 @@
 FEAT = ("x", "zh", "y")
 ALL = MP + FEAT
 LANES = 128
+POSITIONS = 48
 F32 = jnp.float32
 BF16 = jnp.bfloat16
 NT = (((1,), (1,)), ((), ()))
@@ -98,40 +99,28 @@
     members = blocks.shape[0]
     width = members * blocks.shape[2]
     lowered = jnp.concatenate([blocks[i].astype(F32) for i in range(members)], axis=1)
-    scale = heard[:, 2, :]
+    lowered = lowered.astype(BF16)
+    scale = heard[:, 2, 0:POSITIONS]
     high = scale.astype(BF16).astype(F32)
-    low = scale - high
-    both = (high + pltpu.roll(low, LANES // 2, 1)).astype(BF16)
-    lowered = lowered.astype(BF16)
-    half = row.shape[1] // LANES
-    rows = [
-        row[k // half : k // half + 1, (k % half) * LANES : (k % half + 1) * LANES]
-        for k in range(2 * half)
-    ]
-    rows = rows + [jnp.zeros((1, LANES), F32)] * (-len(rows) % heads)
+    flat = jnp.concatenate([row[0:1], row[1:2]], axis=1)
+    columns = width // heads
+    rows = jnp.concatenate(
+        [flat[:, i * columns : (i + 1) * columns] for i in range(heads)], axis=0
+    )
+    tail = jnp.concatenate([high, scale - high, rows], axis=1).astype(BF16)
     for i in range(out.shape[0]):
         out[i, :, 0:width] = lowered
-        out[i, :, width : width + LANES] = both
-    for j in range(len(rows) // heads):
-        some = jnp.concatenate(rows[j * heads : (j + 1) * heads], axis=0).astype(BF16)
-        start = width + (j + 1) * LANES
-        for i in range(out.shape[0]):
-            out[i, :, start : start + LANES] = some
+        out[i, :, width:] = tail
 
 
 def score(position, message, decoder, activation, active, out_hbm, out, sems):
     targets, heads, _ = message.shape
     _, features, width = decoder.shape
     positions = activation.shape[1]
-    count = width // LANES
-    chunks = message[:, :, width + LANES :].astype(F32)
-    direction = jnp.concatenate(
-        [
-            chunks[:, k % heads, (k // heads) * LANES : (k // heads + 1) * LANES]
-            for k in range(count)
-        ],
-        axis=1,
-    ).astype(BF16)
+    columns = width // heads
+    tail = message[:, :, width:].astype(F32)
+    chunks = tail[:, :, 2 * positions : 2 * positions + columns]
+    direction = jnp.concatenate([chunks[:, i, :] for i in range(heads)], axis=1).astype(BF16)
     lowered = message[:, :, 0:width].reshape(targets * heads, width)
     both = jnp.concatenate([lowered, direction], axis=0)
     bottom = lax.dot_general(both, decoder[0], NT, preferred_element_type=F32)
@@ -142,7 +131,7 @@
     per_head_low = per_head - per_head_high
     own_high = own.astype(BF16).astype(F32)
     own_low = own - own_high
-    scale = message[:, :, width : width + LANES].astype(F32)
+    scale = tail[:, :, 0:LANES]
     key = lax.broadcasted_iota(jnp.int32, (heads, LANES), 1)
     below_two = lax.broadcasted_iota(jnp.int32, (heads, LANES), 0) < 2
     spare = jnp.zeros((heads - 2, features), F32)
@@ -150,7 +139,7 @@
     copies = []
     for g in range(targets):
         high = scale[g]
-        low = pltpu.roll(high, LANES // 2, 1)
+        low = pltpu.roll(high, LANES - positions, 1)
         here = jnp.where(below_two & (key == position[g]), 1.0, 0.0)
         mine = slice(g * heads, (g + 1) * heads)
         left = jnp.concatenate([high, low, high, here], axis=0)[:, 0:positions].astype(BF16)
@@ -195,7 +184,6 @@
 ):
     vocab_rows, width = unembed.shape
     targets = target_ids.shape[0]
-    tiles = width // LANES
     columns = w_value.shape[1]
     heads = lax.axis_size(MP)
     first_row = lax.axis_index(ALL) * vocab_rows
@@ -228,7 +216,7 @@
         "lower_block",
     )(block, heard, w_value, norm_gain)
     blocks = lax.all_to_all(blocks, MP, 0, 0, tiled=True)
-    length = width + LANES + -(-tiles // heads) * LANES
+    length = width + 2 * POSITIONS + columns
     message = call(
         build_message, shape((targets, heads, length), BF16), [VMEM, VMEM, VMEM], "build_message"
     )(blocks, heard, row)

time: 82.3 us -> 82.2 us (level)
  no operation moved by 1% of the time
where the time goes in v6:
time: 82.2 us; the launch traced here: 81.9 us
  blocking collectives  75.7 us (92%)
  Pallas kernels  3.86 us (5%)
  local copies, waits for them, and re-layouts  1.26 us (2%)
  matrix products  0.96 us (1%)
    all_to_all x1, blocking collectives, on_device(): parts = lax.all_to_all(parts, ('zl', 'zh'), 0, 0, tiled=True)  25.2 us
    all_to_all x1, blocking collectives, on_device(): parts = lax.all_to_all(found, ('x', 'y', 'core'), 0, 0, tiled=True)  17.6 us
    all_to_all x1, blocking collectives, on_device(): message = lax.all_to_all(message, ('x', 'y'), 0, 0, tiled=True)  14.4 us
    all_to_all x1, blocking collectives, on_device(): heard = lax.all_to_all(asked, MP, 0, 0, tiled=True)  10.1 us
    all_to_all x1, blocking collectives, on_device(): blocks = lax.all_to_all(blocks, MP, 0, 0, tiled=True)  8.29 us
    pallas_call x1, Pallas kernels, on_device(): pl.pallas_call(score, out_shape=shape(activation.shape, F32), in_specs=[S...  2.34 us

profile of v6, /device:TPU:1, one launch (start us, length us, event | category | flops | bytes accessed | tf_op | source)
XLA Modules:
  0.0 81.9 jit_solution(9428037234539583168)
XLA Ops:
  0.0 0.0 copy-start
  0.0 0.0 copy-start.9
  0.0 0.0 copy-start.2
  0.0 0.0 copy-start.8
  0.0 0.0 copy-start.6
  0.1 1.2 %copy-done = bf16[250,2304]{1,0:T(8,128)(2,1)S(1)} copy-done((bf16[250,2304]{1,0:T(8,128)(2,1)S(1)}, bf16[250,2304]{1,0:T(8,128)(2,1)}, u32[]{:S(2)}) %copy-start) | copy-done | bytes 1152024
  1.3 1.0 %fusion.found = f32[16,2304]{1,0:T(8,128)S(1)} fusion(bf16[250,2304]{1,0:T(8,128)(2,1)S(1)} %copy-done, s32[250]{0:T(256)S(1)} %iota_add_fusion, s32[16]{0:T(128)} %param.11), kind=kOutput, calls=%fused_computation | convolution fusion | flops 18436000 | bytes 1300520 | tf_op jit(solution)/shard_map/dot_general | solution.py:195
  2.2 0.1 share_rows.1
  2.4 0.0 copy-start.4
  2.4 0.0 copy-start.7
  2.4 17.6 %all_to_all.25.parts = bf16[32,2,1152]{2,1,0:T(2,128)(2,1)S(1)} all-to-all(bf16[32,2,1152]{2,1,0:T(2,128)(2,1)S(1)} %share_rows.1), channel_id=1, replica_groups=mesh['zl'=4,'core'=2,'x'=4,'zh'=4,'y'=4] {'x','y','core'}, dimensions={0} | all-to-all | bytes 294912 | tf_op jit(solution)/shard_map/all_to_all | solution.py:199
  20.0 0.1 sum_and_repeat.1
  20.0 25.2 %all_to_all.26.parts = bf16[16,2,1152]{2,1,0:T(2,128)(2,1)S(1)} all-to-all(bf16[16,2,1152]{2,1,0:T(2,128)(2,1)S(1)} %sum_and_repeat.1), channel_id=1, replica_groups=mesh['zl'=4,'core'=2,'x'=4,'zh'=4,'y'=4] {'zl','zh'}, dimensions={0} | all-to-all | bytes 147456 | tf_op jit(solution)/shard_map/all_to_all | solution.py:204
  45.3 0.0 copy-done.9
  45.3 0.0 copy-done.2
  45.3 0.0 copy-done.8
  45.3 0.0 copy-done.6
  45.3 0.9 %query_gradient.1 = (f32[2,1152]{1,0:T(2,128)S(1)}, f32[8,8,128]{2,1,0:T(8,128)S(1)}) custom-call(s32[16]{0:T(128)S(1)} %copy-done.9, s32[1]{0:T(128)} %bitcast.1.target, bf16[16,2,1152]{2,1,0:T(2,128)(2,1)S(1)} %all_to_all.26.parts, bf16[256,2304]{1,0:T(8,128)(2,1)S(1)} %bitcast.5, f32[16,48,48]{2,1,0:T(8,128)S(1)} %bitcast.6, f32[16,48]{1,0:T(8,128)S(1)} %copy-done.8), custom_call_target="tpu_custom_call" | custom-call | tf_op jit(solution)/shard_map/query_gradient/pallas_call | solution.py:205
  46.2 0.0 copy-start.5
  46.2 10.1 %all_to_all.27.heard = f32[8,8,128]{2,1,0:T(8,128)S(1)} all-to-all(f32[8,8,128]{2,1,0:T(8,128)S(1)} %get-tuple-element.7), channel_id=1, replica_groups=mesh['zl'=4,'core'=2,'x'=4,'zh'=4,'y'=4] {'zl','core'}, dimensions={0} | all-to-all | bytes 65536 | tf_op jit(solution)/shard_map/all_to_all | solution.py:211
  56.3 0.0 copy-done.4
  56.3 0.0 copy-done.7
  56.3 0.0 copy-start.3
  56.3 0.3 lower_block.1
  56.6 0.0 copy-start.1
  56.6 8.3 %all_to_all.28.blocks = bf16[8,8,288]{2,1,0:T(8,128)(2,1)S(1)} all-to-all(bf16[8,8,288]{2,1,0:T(8,128)(2,1)S(1)} %lower_block.1), channel_id=1, replica_groups=mesh['zl'=4,'core'=2,'x'=4,'zh'=4,'y'=4] {'zl','core'}, dimensions={0} | all-to-all | bytes 73728 | tf_op jit(solution)/shard_map/all_to_all | solution.py:218
  64.9 0.2 build_message.1
  65.1 14.4 %all_to_all.29.message = bf16[16,8,2688]{2,1,0:T(8,128)(2,1)S(1)} all-to-all(bf16[16,8,2688]{2,1,0:T(8,128)(2,1)S(1)} %build_message.1), channel_id=1, replica_groups=mesh['zl'=4,'core'=2,'x'=4,'zh'=4,'y'=4] {'x','y'}, dimensions={0} | all-to-all | bytes 1376256 | tf_op jit(solution)/shard_map/all_to_all | solution.py:223
  79.5 0.0 copy-done.5
  79.5 0.0 copy-done.3
  79.5 0.0 copy-done.1
  79.5 2.3 %score.1 = f32[16,48,192]{2,1,0:T(8,128)} custom-call(s32[16]{0:T(128)S(1)} %copy-done.9, bf16[16,8,2688]{2,1,0:T(8,128)(2,1)S(1)} %all_to_all.29.message, bf16[2,192,2304]{2,1,0:T(8,128)(2,1)S(1)} %copy-done.1, bf16[16,48,192]{2,1,0:T(8,128)(2,1)S(1)} %copy-done.5, s32[16,48,192]{2,1,0:T(8,128)S(1)} %copy-done.3), custom_call_target="tpu_custom_call" | custom-call | tf_op jit(solution)/shard_map/score/pallas_call | solution.py:224
  (1 shorter events, 0.0 us)
Async XLA Ops:
  0.0 1.3 %copy-start = (bf16[250,2304]{1,0:T(8,128)(2,1)S(1)}, bf16[250,2304]{1,0:T(8,128)(2,1)}, u32[]{:S(2)}) copy-start(bf16[250,2304]{1,0:T(8,128)(2,1)} %param.13) | copy-start | bytes 3456004
  0.0 45.3 %copy-start.9 = (s32[16]{0:T(128)S(1)}, s32[16]{0:T(128)}, u32[]{:S(2)}) copy-start(s32[16]{0:T(128)} %position.3) | copy-start | bytes 196
  0.0 45.3 %copy-start.2 = (bf16[1,256,2304]{2,1,0:T(8,128)(2,1)S(1)}, bf16[1,256,2304]{2,1,0:T(8,128)(2,1)}, u32[]{:S(2)}) copy-start(bf16[1,256,2304]{2,1,0:T(8,128)(2,1)} %param.18) | copy-start | bytes 3538948
  0.0 45.3 %copy-start.8 = (f32[16,48]{1,0:T(8,128)S(1)}, f32[16,48]{1,0:T(8,128)}, u32[]{:S(2)}) copy-start(f32[16,48]{1,0:T(8,128)} %inv_rms.1) | copy-start | bytes 9220
  0.0 45.3 %copy-start.6 = (f32[1,16,48,48]{3,2,1,0:T(8,128)S(1)}, f32[1,16,48,48]{3,2,1,0:T(8,128)}, u32[]{:S(2)}) copy-start(f32[1,16,48,48]{3,2,1,0:T(8,128)} %param.14) | copy-start | bytes 442372
  2.4 54.0 %copy-start.4 = (bf16[4,288,256]{2,1,0:T(8,128)(2,1)S(1)}, bf16[4,288,256]{2,1,0:T(8,128)(2,1)}, u32[]{:S(2)}) copy-start(bf16[4,288,256]{2,1,0:T(8,128)(2,1)} %w_value.1) | copy-start | bytes 1769476
  2.4 54.0 %copy-start.7 = (f32[2304]{0:T(1024)S(1)}, f32[2304]{0:T(1024)}, u32[]{:S(2)}) copy-start(f32[2304]{0:T(1024)} %gain.1) | copy-start | bytes 27652
  46.2 33.3 %copy-start.5 = (bf16[16,48,192]{2,1,0:T(8,128)(2,1)S(1)}, bf16[16,48,192]{2,1,0:T(8,128)(2,1)}, u32[]{:S(2)}) copy-start(bf16[16,48,192]{2,1,0:T(8,128)(2,1)} %activation.1) | copy-start | bytes 884740
  56.3 23.2 %copy-start.3 = (s32[16,48,192]{2,1,0:T(8,128)S(1)}, s32[16,48,192]{2,1,0:T(8,128)}, u32[]{:S(2)}) copy-start(s32[16,48,192]{2,1,0:T(8,128)} %active.1) | copy-start | bytes 1769476
  56.6 22.9 %copy-start.1 = (bf16[2,192,2304]{2,1,0:T(8,128)(2,1)S(1)}, bf16[2,192,2304]{2,1,0:T(8,128)(2,1)}, u32[]{:S(2)}) copy-start(bf16[2,192,2304]{2,1,0:T(8,128)(2,1)} %decoder.1) | copy-start | bytes 5308420

commit v7 on v6

--- a/solution.py
+++ b/solution.py
@@ -68,17 +68,22 @@
     scale = weights / jnp.sum(weights, axis=1, keepdims=True)
     scale = scale * inv_rms[pl.ds(target[0], 1), :]
     positions = weights.shape[1]
-    for i in range(out.shape[0]):
-        for k in range(gradient.shape[1] // LANES):
-            out[i, k : k + 1, :] = gradient[:, k * LANES : (k + 1) * LANES]
-        out[i, 2:3, 0:positions] = scale
-        out[i, 2:3, positions:] = jnp.zeros((1, LANES - positions), F32)
+    count = gradient.shape[1] // LANES
+    high = scale.astype(BF16).astype(F32)
+    gap = jnp.zeros((1, LANES - positions), F32)
+    lines = [gradient[:, k * LANES : (k + 1) * LANES] for k in range(count)]
+    lines += [jnp.concatenate([part, gap], axis=1) for part in (high, scale - high)]
+    lines.append(jnp.zeros((out.shape[1] - len(lines), LANES), F32))
+    message = jnp.concatenate(lines, axis=0).astype(BF16)
+    for i in range(out.shape[0]):
+        out[i] = message
 
 
 def lower_block(block, heard, w_value, gain, out):
     heads = heard.shape[0]
     kv_heads, columns, _ = w_value.shape
-    gradient = jnp.concatenate([heard[:, 0, :], heard[:, 1, :]], axis=1).astype(BF16)
+    rows = heard[...].astype(F32)
+    gradient = jnp.concatenate([rows[:, 0, :], rows[:, 1, :]], axis=1).astype(BF16)
     head = lax.broadcasted_iota(jnp.int32, (heads, columns), 0)
     lowered = jnp.zeros((heads, columns), F32)
     for v in range(kv_heads):
@@ -100,14 +105,15 @@
     width = members * blocks.shape[2]
     lowered = jnp.concatenate([blocks[i].astype(F32) for i in range(members)], axis=1)
     lowered = lowered.astype(BF16)
-    scale = heard[:, 2, 0:POSITIONS]
-    high = scale.astype(BF16).astype(F32)
+    asked = heard[...].astype(F32)
+    high = asked[:, 2, 0:POSITIONS]
+    low = asked[:, 3, 0:POSITIONS]
     flat = jnp.concatenate([row[0:1], row[1:2]], axis=1)
     columns = width // heads
     rows = jnp.concatenate(
         [flat[:, i * columns : (i + 1) * columns] for i in range(heads)], axis=0
     )
-    tail = jnp.concatenate([high, scale - high, rows], axis=1).astype(BF16)
+    tail = jnp.concatenate([high, low, rows], axis=1).astype(BF16)
     for i in range(out.shape[0]):
         out[i, :, 0:width] = lowered
         out[i, :, width:] = tail
@@ -124,7 +130,7 @@
     lowered = message[:, :, 0:width].reshape(targets * heads, width)
     both = jnp.concatenate([lowered, direction], axis=0)
     bottom = lax.dot_general(both, decoder[0], NT, preferred_element_type=F32)
-    top = lax.dot_general(direction, decoder[1], NT, preferred_element_type=F32)
+    top = lax.dot_general(decoder[1], direction, NT, preferred_element_type=F32).T
     per_head = bottom[0 : targets * heads]
     own = bottom[targets * heads :] + top
     per_head_high = per_head.astype(BF16).astype(F32)
@@ -135,7 +141,7 @@
     key = lax.broadcasted_iota(jnp.int32, (heads, LANES), 1)
     below_two = lax.broadcasted_iota(jnp.int32, (heads, LANES), 0) < 2
     spare = jnp.zeros((heads - 2, features), F32)
-    step = targets // 4
+    step = targets // 8
     copies = []
     for g in range(targets):
         high = scale[g]
@@ -204,7 +210,7 @@
     parts = lax.all_to_all(parts, ("zl", "zh"), 0, 0, tiled=True)
     row, asked = call(
         query_gradient,
-        (shape((2, width // 2), F32), shape((heads, 8, LANES), F32)),
+        (shape((2, width // 2), F32), shape((heads, 8, LANES), BF16)),
         [SMEM, SMEM, VMEM, VMEM, VMEM, VMEM],
         "query_gradient",
     )(target_pos, target, parts, w_out[0], attn_weights[0], inv_rms)
@@ -226,7 +232,7 @@
         out_shape=shape(activation.shape, F32),
         in_specs=[SMEM, VMEM, VMEM, VMEM, VMEM],
         out_specs=HBM,
-        scratch_shapes=[pltpu.VMEM(activation.shape, F32), pltpu.SemaphoreType.DMA((4,))],
+        scratch_shapes=[pltpu.VMEM(activation.shape, F32), pltpu.SemaphoreType.DMA((8,))],
         name="score",
         compiler_params=pltpu.CompilerParams(vmem_limit_bytes=32 * 1024 * 1024),
     )(target_pos, message, decoder, activation, active)

time: 82.2 us -> 82.1 us (level)
  no operation moved by 1% of the time
where the time goes in v7:
time: 82.1 us; the launch traced here: 81.7 us
  blocking collectives  75.5 us (92%)
  Pallas kernels  3.92 us (5%)
  local copies, waits for them, and re-layouts  1.26 us (2%)
  matrix products  0.96 us (1%)
    all_to_all x1, blocking collectives, on_device(): parts = lax.all_to_all(parts, ('zl', 'zh'), 0, 0, tiled=True)  25.2 us
    all_to_all x1, blocking collectives, on_device(): parts = lax.all_to_all(found, ('x', 'y', 'core'), 0, 0, tiled=True)  17.6 us
    all_to_all x1, blocking collectives, on_device(): message = lax.all_to_all(message, ('x', 'y'), 0, 0, tiled=True)  14.4 us
    all_to_all x1, blocking collectives, on_device(): heard = lax.all_to_all(asked, MP, 0, 0, tiled=True)  9.94 us
    all_to_all x1, blocking collectives, on_device(): blocks = lax.all_to_all(blocks, MP, 0, 0, tiled=True)  8.25 us
    pallas_call x1, Pallas kernels, on_device(): pl.pallas_call(score, out_shape=shape(activation.shape, F32), in_specs=[S...  2.38 us

profile of v7, /device:TPU:1, one launch (start us, length us, event | category | flops | bytes accessed | tf_op | source)
XLA Modules:
  0.0 81.7 jit_solution(11711813830941831148)
XLA Ops:
  0.0 0.0 copy-start
  0.0 0.0 copy-start.9
  0.0 0.0 copy-start.2
  0.0 0.0 copy-start.8
  0.0 0.0 copy-start.6
  0.1 1.2 %copy-done = bf16[250,2304]{1,0:T(8,128)(2,1)S(1)} copy-done((bf16[250,2304]{1,0:T(8,128)(2,1)S(1)}, bf16[250,2304]{1,0:T(8,128)(2,1)}, u32[]{:S(2)}) %copy-start) | copy-done | bytes 1152024
  1.3 1.0 %fusion.found = f32[16,2304]{1,0:T(8,128)S(1)} fusion(bf16[250,2304]{1,0:T(8,128)(2,1)S(1)} %copy-done, s32[250]{0:T(256)S(1)} %iota_add_fusion, s32[16]{0:T(128)} %param.11), kind=kOutput, calls=%fused_computation | convolution fusion | flops 18436000 | bytes 1300520 | tf_op jit(solution)/shard_map/dot_general | solution.py:201
  2.2 0.1 share_rows.1
  2.4 0.0 copy-start.4
  2.4 0.0 copy-start.7
  2.4 17.6 %all_to_all.25.parts = bf16[32,2,1152]{2,1,0:T(2,128)(2,1)S(1)} all-to-all(bf16[32,2,1152]{2,1,0:T(2,128)(2,1)S(1)} %share_rows.1), channel_id=1, replica_groups=mesh['zl'=4,'core'=2,'x'=4,'zh'=4,'y'=4] {'x','y','core'}, dimensions={0} | all-to-all | bytes 294912 | tf_op jit(solution)/shard_map/all_to_all | solution.py:205
  20.0 0.1 sum_and_repeat.1
  20.0 25.2 %all_to_all.26.parts = bf16[16,2,1152]{2,1,0:T(2,128)(2,1)S(1)} all-to-all(bf16[16,2,1152]{2,1,0:T(2,128)(2,1)S(1)} %sum_and_repeat.1), channel_id=1, replica_groups=mesh['zl'=4,'core'=2,'x'=4,'zh'=4,'y'=4] {'zl','zh'}, dimensions={0} | all-to-all | bytes 147456 | tf_op jit(solution)/shard_map/all_to_all | solution.py:210
  45.3 0.0 copy-done.9
  45.3 0.0 copy-done.2
  45.3 0.0 copy-done.8
  45.3 0.0 copy-done.6
  45.3 0.0 copy-start.5
  45.3 0.9 %query_gradient.1 = (f32[2,1152]{1,0:T(2,128)S(1)}, bf16[8,8,128]{2,1,0:T(8,128)(2,1)S(1)}) custom-call(s32[16]{0:T(128)S(1)} %copy-done.9, s32[1]{0:T(128)} %bitcast.1.target, bf16[16,2,1152]{2,1,0:T(2,128)(2,1)S(1)} %all_to_all.26.parts, bf16[256,2304]{1,0:T(8,128)(2,1)S(1)} %bitcast.5, f32[16,48,48]{2,1,0:T(8,128)S(1)} %bitcast.6, f32[16,48]{1,0:T(8,128)S(1)} %copy-done.8), custom_call_target="tpu_custom_call" | custom-call | tf_op jit(solution)/shard_map/query_gradient/pallas_call | solution.py:211
  46.2 9.9 %all_to_all.27.heard = bf16[8,8,128]{2,1,0:T(8,128)(2,1)S(1)} all-to-all(bf16[8,8,128]{2,1,0:T(8,128)(2,1)S(1)} %get-tuple-element.7), channel_id=1, replica_groups=mesh['zl'=4,'core'=2,'x'=4,'zh'=4,'y'=4] {'zl','core'}, dimensions={0} | all-to-all | bytes 32768 | tf_op jit(solution)/shard_map/all_to_all | solution.py:217
  56.2 0.0 copy-done.4
  56.2 0.0 copy-done.7
  56.2 0.0 copy-start.3
  56.2 0.3 lower_block.1
  56.4 0.0 copy-start.1
  56.5 8.2 %all_to_all.28.blocks = bf16[8,8,288]{2,1,0:T(8,128)(2,1)S(1)} all-to-all(bf16[8,8,288]{2,1,0:T(8,128)(2,1)S(1)} %lower_block.1), channel_id=1, replica_groups=mesh['zl'=4,'core'=2,'x'=4,'zh'=4,'y'=4] {'zl','core'}, dimensions={0} | all-to-all | bytes 73728 | tf_op jit(solution)/shard_map/all_to_all | solution.py:224
  64.7 0.2 build_message.1
  64.9 14.4 %all_to_all.29.message = bf16[16,8,2688]{2,1,0:T(8,128)(2,1)S(1)} all-to-all(bf16[16,8,2688]{2,1,0:T(8,128)(2,1)S(1)} %build_message.1), channel_id=1, replica_groups=mesh['zl'=4,'core'=2,'x'=4,'zh'=4,'y'=4] {'x','y'}, dimensions={0} | all-to-all | bytes 1376256 | tf_op jit(solution)/shard_map/all_to_all | solution.py:229
  79.3 0.0 copy-done.5
  79.3 0.0 copy-done.3
  79.3 0.0 copy-done.1
  79.4 2.4 %score.1 = f32[16,48,192]{2,1,0:T(8,128)} custom-call(s32[16]{0:T(128)S(1)} %copy-done.9, bf16[16,8,2688]{2,1,0:T(8,128)(2,1)S(1)} %all_to_all.29.message, bf16[2,192,2304]{2,1,0:T(8,128)(2,1)S(1)} %copy-done.1, bf16[16,48,192]{2,1,0:T(8,128)(2,1)S(1)} %copy-done.5, s32[16,48,192]{2,1,0:T(8,128)S(1)} %copy-done.3), custom_call_target="tpu_custom_call" | custom-call | tf_op jit(solution)/shard_map/score/pallas_call | solution.py:230
  (1 shorter events, 0.0 us)
Async XLA Ops:
  0.0 1.3 %copy-start = (bf16[250,2304]{1,0:T(8,128)(2,1)S(1)}, bf16[250,2304]{1,0:T(8,128)(2,1)}, u32[]{:S(2)}) copy-start(bf16[250,2304]{1,0:T(8,128)(2,1)} %param.13) | copy-start | bytes 3456004
  0.0 45.3 %copy-start.9 = (s32[16]{0:T(128)S(1)}, s32[16]{0:T(128)}, u32[]{:S(2)}) copy-start(s32[16]{0:T(128)} %position.3) | copy-start | bytes 196
  0.0 45.3 %copy-start.2 = (bf16[1,256,2304]{2,1,0:T(8,128)(2,1)S(1)}, bf16[1,256,2304]{2,1,0:T(8,128)(2,1)}, u32[]{:S(2)}) copy-start(bf16[1,256,2304]{2,1,0:T(8,128)(2,1)} %param.18) | copy-start | bytes 3538948
  0.0 45.3 %copy-start.8 = (f32[16,48]{1,0:T(8,128)S(1)}, f32[16,48]{1,0:T(8,128)}, u32[]{:S(2)}) copy-start(f32[16,48]{1,0:T(8,128)} %inv_rms.1) | copy-start | bytes 9220
  0.0 45.3 %copy-start.6 = (f32[1,16,48,48]{3,2,1,0:T(8,128)S(1)}, f32[1,16,48,48]{3,2,1,0:T(8,128)}, u32[]{:S(2)}) copy-start(f32[1,16,48,48]{3,2,1,0:T(8,128)} %param.14) | copy-start | bytes 442372
  2.4 53.8 %copy-start.4 = (bf16[4,288,256]{2,1,0:T(8,128)(2,1)S(1)}, bf16[4,288,256]{2,1,0:T(8,128)(2,1)}, u32[]{:S(2)}) copy-start(bf16[4,288,256]{2,1,0:T(8,128)(2,1)} %w_value.1) | copy-start | bytes 1769476
  2.4 53.8 %copy-start.7 = (f32[2304]{0:T(1024)S(1)}, f32[2304]{0:T(1024)}, u32[]{:S(2)}) copy-start(f32[2304]{0:T(1024)} %gain.1) | copy-start | bytes 27652
  45.3 34.1 %copy-start.5 = (bf16[16,48,192]{2,1,0:T(8,128)(2,1)S(1)}, bf16[16,48,192]{2,1,0:T(8,128)(2,1)}, u32[]{:S(2)}) copy-start(bf16[16,48,192]{2,1,0:T(8,128)(2,1)} %activation.1) | copy-start | bytes 884740
  56.2 23.2 %copy-start.3 = (s32[16,48,192]{2,1,0:T(8,128)S(1)}, s32[16,48,192]{2,1,0:T(8,128)}, u32[]{:S(2)}) copy-start(s32[16,48,192]{2,1,0:T(8,128)} %active.1) | copy-start | bytes 1769476
  56.4 22.9 %copy-start.1 = (bf16[2,192,2304]{2,1,0:T(8,128)(2,1)S(1)}, bf16[2,192,2304]{2,1,0:T(8,128)(2,1)}, u32[]{:S(2)}) copy-start(bf16[2,192,2304]{2,1,0:T(8,128)(2,1)} %decoder.1) | copy-start | bytes 5308420

commit v8 on v7

--- a/solution.py
+++ b/solution.py
@@ -203,11 +203,11 @@
         share_rows, shape((2 * targets, 2, width // 2), BF16), [SMEM, SMEM, VMEM], "share_rows"
     )(target, block, found)
     parts = lax.all_to_all(found, ("x", "y", "core"), 0, 0, tiled=True)
-    ring = lax.axis_size(("zl", "zh"))
+    ring = lax.axis_size(("zh", "zl"))
     parts = call(
         sum_and_repeat, shape((ring, 2, width // 2), BF16), [VMEM], "sum_and_repeat"
     )(parts)
-    parts = lax.all_to_all(parts, ("zl", "zh"), 0, 0, tiled=True)
+    parts = lax.all_to_all(parts, ("zh", "zl"), 0, 0, tiled=True)
     row, asked = call(
         query_gradient,
         (shape((2, width // 2), F32), shape((heads, 8, LANES), BF16)),

time: 82.1 us -> 81.7 us (level)
  no operation moved by 1% of the time
where the time goes in v8:
time: 81.7 us; the launch traced here: 81.3 us
  blocking collectives  75.1 us (92%)
  Pallas kernels  3.92 us (5%)
  local copies, waits for them, and re-layouts  1.26 us (2%)
  matrix products  0.96 us (1%)
    all_to_all x1, blocking collectives, on_device(): parts = lax.all_to_all(parts, ('zh', 'zl'), 0, 0, tiled=True)  25.2 us
    all_to_all x1, blocking collectives, on_device(): parts = lax.all_to_all(found, ('x', 'y', 'core'), 0, 0, tiled=True)  17.6 us
    all_to_all x1, blocking collectives, on_device(): message = lax.all_to_all(message, ('x', 'y'), 0, 0, tiled=True)  14.4 us
    all_to_all x1, blocking collectives, on_device(): heard = lax.all_to_all(asked, MP, 0, 0, tiled=True)  9.57 us
    all_to_all x1, blocking collectives, on_device(): blocks = lax.all_to_all(blocks, MP, 0, 0, tiled=True)  8.25 us
    pallas_call x1, Pallas kernels, on_device(): pl.pallas_call(score, out_shape=shape(activation.shape, F32), in_specs=[S...  2.38 us

profile of v8, /device:TPU:1, one launch (start us, length us, event | category | flops | bytes accessed | tf_op | source)
XLA Modules:
  0.0 81.3 jit_solution(5226867785942577138)
XLA Ops:
  0.0 0.0 copy-start
  0.0 0.0 copy-start.9
  0.0 0.0 copy-start.2
  0.0 0.0 copy-start.8
  0.0 0.0 copy-start.6
  0.1 1.2 %copy-done = bf16[250,2304]{1,0:T(8,128)(2,1)S(1)} copy-done((bf16[250,2304]{1,0:T(8,128)(2,1)S(1)}, bf16[250,2304]{1,0:T(8,128)(2,1)}, u32[]{:S(2)}) %copy-start) | copy-done | bytes 1152024
  1.3 1.0 %fusion.found = f32[16,2304]{1,0:T(8,128)S(1)} fusion(bf16[250,2304]{1,0:T(8,128)(2,1)S(1)} %copy-done, s32[250]{0:T(256)S(1)} %iota_add_fusion, s32[16]{0:T(128)} %param.11), kind=kOutput, calls=%fused_computation | convolution fusion | flops 18436000 | bytes 1300520 | tf_op jit(solution)/shard_map/dot_general | solution.py:201
  2.2 0.1 share_rows.1
  2.4 0.0 copy-start.4
  2.4 0.0 copy-start.7
  2.4 17.6 %all_to_all.25.parts = bf16[32,2,1152]{2,1,0:T(2,128)(2,1)S(1)} all-to-all(bf16[32,2,1152]{2,1,0:T(2,128)(2,1)S(1)} %share_rows.1), channel_id=1, replica_groups=mesh['zl'=4,'core'=2,'x'=4,'zh'=4,'y'=4] {'x','y','core'}, dimensions={0} | all-to-all | bytes 294912 | tf_op jit(solution)/shard_map/all_to_all | solution.py:205
  20.0 0.1 sum_and_repeat.1
  20.0 25.2 %all_to_all.26.parts = bf16[16,2,1152]{2,1,0:T(2,128)(2,1)S(1)} all-to-all(bf16[16,2,1152]{2,1,0:T(2,128)(2,1)S(1)} %sum_and_repeat.1), channel_id=1, replica_groups=mesh['zl'=4,'core'=2,'x'=4,'zh'=4,'y'=4] {'zh','zl'}, dimensions={0} | all-to-all | bytes 147456 | tf_op jit(solution)/shard_map/all_to_all | solution.py:210
  45.2 0.0 copy-done.9
  45.2 0.0 copy-done.2
  45.2 0.0 copy-done.8
  45.2 0.0 copy-done.6
  45.3 0.0 copy-start.5
  45.3 0.9 %query_gradient.1 = (f32[2,1152]{1,0:T(2,128)S(1)}, bf16[8,8,128]{2,1,0:T(8,128)(2,1)S(1)}) custom-call(s32[16]{0:T(128)S(1)} %copy-done.9, s32[1]{0:T(128)} %bitcast.1.target, bf16[16,2,1152]{2,1,0:T(2,128)(2,1)S(1)} %all_to_all.26.parts, bf16[256,2304]{1,0:T(8,128)(2,1)S(1)} %bitcast.5, f32[16,48,48]{2,1,0:T(8,128)S(1)} %bitcast.6, f32[16,48]{1,0:T(8,128)S(1)} %copy-done.8), custom_call_target="tpu_custom_call" | custom-call | tf_op jit(solution)/shard_map/query_gradient/pallas_call | solution.py:211
  46.2 9.6 %all_to_all.27.heard = bf16[8,8,128]{2,1,0:T(8,128)(2,1)S(1)} all-to-all(bf16[8,8,128]{2,1,0:T(8,128)(2,1)S(1)} %get-tuple-element.7), channel_id=1, replica_groups=mesh['zl'=4,'core'=2,'x'=4,'zh'=4,'y'=4] {'zl','core'}, dimensions={0} | all-to-all | bytes 32768 | tf_op jit(solution)/shard_map/all_to_all | solution.py:217
  55.8 0.0 copy-done.4
  55.8 0.0 copy-done.7
  55.8 0.0 copy-start.3
  55.8 0.3 lower_block.1
  56.0 0.0 copy-start.1
  56.1 8.2 %all_to_all.28.blocks = bf16[8,8,288]{2,1,0:T(8,128)(2,1)S(1)} all-to-all(bf16[8,8,288]{2,1,0:T(8,128)(2,1)S(1)} %lower_block.1), channel_id=1, replica_groups=mesh['zl'=4,'core'=2,'x'=4,'zh'=4,'y'=4] {'zl','core'}, dimensions={0} | all-to-all | bytes 73728 | tf_op jit(solution)/shard_map/all_to_all | solution.py:224
  64.3 0.2 build_message.1
  64.5 14.4 %all_to_all.29.message = bf16[16,8,2688]{2,1,0:T(8,128)(2,1)S(1)} all-to-all(bf16[16,8,2688]{2,1,0:T(8,128)(2,1)S(1)} %build_message.1), channel_id=1, replica_groups=mesh['zl'=4,'core'=2,'x'=4,'zh'=4,'y'=4] {'x','y'}, dimensions={0} | all-to-all | bytes 1376256 | tf_op jit(solution)/shard_map/all_to_all | solution.py:229
  78.9 0.0 copy-done.5
  78.9 0.0 copy-done.3
  78.9 0.0 copy-done.1
  79.0 2.4 %score.1 = f32[16,48,192]{2,1,0:T(8,128)} custom-call(s32[16]{0:T(128)S(1)} %copy-done.9, bf16[16,8,2688]{2,1,0:T(8,128)(2,1)S(1)} %all_to_all.29.message, bf16[2,192,2304]{2,1,0:T(8,128)(2,1)S(1)} %copy-done.1, bf16[16,48,192]{2,1,0:T(8,128)(2,1)S(1)} %copy-done.5, s32[16,48,192]{2,1,0:T(8,128)S(1)} %copy-done.3), custom_call_target="tpu_custom_call" | custom-call | tf_op jit(solution)/shard_map/score/pallas_call | solution.py:230
  (1 shorter events, 0.0 us)
Async XLA Ops:
  0.0 1.3 %copy-start = (bf16[250,2304]{1,0:T(8,128)(2,1)S(1)}, bf16[250,2304]{1,0:T(8,128)(2,1)}, u32[]{:S(2)}) copy-start(bf16[250,2304]{1,0:T(8,128)(2,1)} %param.13) | copy-start | bytes 3456004
  0.0 45.2 %copy-start.9 = (s32[16]{0:T(128)S(1)}, s32[16]{0:T(128)}, u32[]{:S(2)}) copy-start(s32[16]{0:T(128)} %position.3) | copy-start | bytes 196
  0.0 45.2 %copy-start.2 = (bf16[1,256,2304]{2,1,0:T(8,128)(2,1)S(1)}, bf16[1,256,2304]{2,1,0:T(8,128)(2,1)}, u32[]{:S(2)}) copy-start(bf16[1,256,2304]{2,1,0:T(8,128)(2,1)} %param.18) | copy-start | bytes 3538948
  0.0 45.2 %copy-start.8 = (f32[16,48]{1,0:T(8,128)S(1)}, f32[16,48]{1,0:T(8,128)}, u32[]{:S(2)}) copy-start(f32[16,48]{1,0:T(8,128)} %inv_rms.1) | copy-start | bytes 9220
  0.0 45.2 %copy-start.6 = (f32[1,16,48,48]{3,2,1,0:T(8,128)S(1)}, f32[1,16,48,48]{3,2,1,0:T(8,128)}, u32[]{:S(2)}) copy-start(f32[1,16,48,48]{3,2,1,0:T(8,128)} %param.14) | copy-start | bytes 442372
  2.4 53.4 %copy-start.4 = (bf16[4,288,256]{2,1,0:T(8,128)(2,1)S(1)}, bf16[4,288,256]{2,1,0:T(8,128)(2,1)}, u32[]{:S(2)}) copy-start(bf16[4,288,256]{2,1,0:T(8,128)(2,1)} %w_value.1) | copy-start | bytes 1769476
  2.4 53.4 %copy-start.7 = (f32[2304]{0:T(1024)S(1)}, f32[2304]{0:T(1024)}, u32[]{:S(2)}) copy-start(f32[2304]{0:T(1024)} %gain.1) | copy-start | bytes 27652
  45.3 33.7 %copy-start.5 = (bf16[16,48,192]{2,1,0:T(8,128)(2,1)S(1)}, bf16[16,48,192]{2,1,0:T(8,128)(2,1)}, u32[]{:S(2)}) copy-start(bf16[16,48,192]{2,1,0:T(8,128)(2,1)} %activation.1) | copy-start | bytes 884740
  55.8 23.2 %copy-start.3 = (s32[16,48,192]{2,1,0:T(8,128)S(1)}, s32[16,48,192]{2,1,0:T(8,128)}, u32[]{:S(2)}) copy-start(s32[16,48,192]{2,1,0:T(8,128)} %active.1) | copy-start | bytes 1769476
  56.0 22.9 %copy-start.1 = (bf16[2,192,2304]{2,1,0:T(8,128)(2,1)S(1)}, bf16[2,192,2304]{2,1,0:T(8,128)(2,1)}, u32[]{:S(2)}) copy-start(bf16[2,192,2304]{2,1,0:T(8,128)(2,1)} %decoder.1) | copy-start | bytes 5308420

commit v9 on v8

--- a/solution.py
+++ b/solution.py
@@ -141,7 +141,7 @@
     key = lax.broadcasted_iota(jnp.int32, (heads, LANES), 1)
     below_two = lax.broadcasted_iota(jnp.int32, (heads, LANES), 0) < 2
     spare = jnp.zeros((heads - 2, features), F32)
-    step = targets // 8
+    step = targets // 16
     copies = []
     for g in range(targets):
         high = scale[g]
@@ -232,7 +232,7 @@
         out_shape=shape(activation.shape, F32),
         in_specs=[SMEM, VMEM, VMEM, VMEM, VMEM],
         out_specs=HBM,
-        scratch_shapes=[pltpu.VMEM(activation.shape, F32), pltpu.SemaphoreType.DMA((8,))],
+        scratch_shapes=[pltpu.VMEM(activation.shape, F32), pltpu.SemaphoreType.DMA((16,))],
         name="score",
         compiler_params=pltpu.CompilerParams(vmem_limit_bytes=32 * 1024 * 1024),
     )(target_pos, message, decoder, activation, active)

time: 81.7 us -> 81.7 us (level)
  no operation moved by 1% of the time
where the time goes in v9:
time: 81.7 us; the launch traced here: 81.4 us
  blocking collectives  75.1 us (92%)
  Pallas kernels  3.97 us (5%)
  local copies, waits for them, and re-layouts  1.26 us (2%)
  matrix products  0.96 us (1%)
    all_to_all x1, blocking collectives, on_device(): parts = lax.all_to_all(parts, ('zh', 'zl'), 0, 0, tiled=True)  25.2 us
    all_to_all x1, blocking collectives, on_device(): parts = lax.all_to_all(found, ('x', 'y', 'core'), 0, 0, tiled=True)  17.6 us
    all_to_all x1, blocking collectives, on_device(): message = lax.all_to_all(message, ('x', 'y'), 0, 0, tiled=True)  14.4 us
    all_to_all x1, blocking collectives, on_device(): heard = lax.all_to_all(asked, MP, 0, 0, tiled=True)  9.57 us
    all_to_all x1, blocking collectives, on_device(): blocks = lax.all_to_all(blocks, MP, 0, 0, tiled=True)  8.25 us
    pallas_call x1, Pallas kernels, on_device(): pl.pallas_call(score, out_shape=shape(activation.shape, F32), in_specs=[S...  2.43 us

profile of v9, /device:TPU:1, one launch (start us, length us, event | category | flops | bytes accessed | tf_op | source)
XLA Modules:
  0.0 81.4 jit_solution(8508789670054456652)
XLA Ops:
  0.0 0.0 copy-start
  0.0 0.0 copy-start.9
  0.0 0.0 copy-start.2
  0.0 0.0 copy-start.8
  0.0 0.0 copy-start.6
  0.1 1.2 %copy-done = bf16[250,2304]{1,0:T(8,128)(2,1)S(1)} copy-done((bf16[250,2304]{1,0:T(8,128)(2,1)S(1)}, bf16[250,2304]{1,0:T(8,128)(2,1)}, u32[]{:S(2)}) %copy-start) | copy-done | bytes 1152024
  1.3 1.0 %fusion.found = f32[16,2304]{1,0:T(8,128)S(1)} fusion(bf16[250,2304]{1,0:T(8,128)(2,1)S(1)} %copy-done, s32[250]{0:T(256)S(1)} %iota_add_fusion, s32[16]{0:T(128)} %param.11), kind=kOutput, calls=%fused_computation | convolution fusion | flops 18436000 | bytes 1300520 | tf_op jit(solution)/shard_map/dot_general | solution.py:201
  2.2 0.1 share_rows.1
  2.4 0.0 copy-start.4
  2.4 0.0 copy-start.7
  2.4 17.6 %all_to_all.25.parts = bf16[32,2,1152]{2,1,0:T(2,128)(2,1)S(1)} all-to-all(bf16[32,2,1152]{2,1,0:T(2,128)(2,1)S(1)} %share_rows.1), channel_id=1, replica_groups=mesh['zl'=4,'core'=2,'x'=4,'zh'=4,'y'=4] {'x','y','core'}, dimensions={0} | all-to-all | bytes 294912 | tf_op jit(solution)/shard_map/all_to_all | solution.py:205
  20.0 0.1 sum_and_repeat.1
  20.0 25.2 %all_to_all.26.parts = bf16[16,2,1152]{2,1,0:T(2,128)(2,1)S(1)} all-to-all(bf16[16,2,1152]{2,1,0:T(2,128)(2,1)S(1)} %sum_and_repeat.1), channel_id=1, replica_groups=mesh['zl'=4,'core'=2,'x'=4,'zh'=4,'y'=4] {'zh','zl'}, dimensions={0} | all-to-all | bytes 147456 | tf_op jit(solution)/shard_map/all_to_all | solution.py:210
  45.2 0.0 copy-done.9
  45.2 0.0 copy-done.2
  45.2 0.0 copy-done.8
  45.2 0.0 copy-done.6
  45.3 0.0 copy-start.5
  45.3 0.9 %query_gradient.1 = (f32[2,1152]{1,0:T(2,128)S(1)}, bf16[8,8,128]{2,1,0:T(8,128)(2,1)S(1)}) custom-call(s32[16]{0:T(128)S(1)} %copy-done.9, s32[1]{0:T(128)} %bitcast.1.target, bf16[16,2,1152]{2,1,0:T(2,128)(2,1)S(1)} %all_to_all.26.parts, bf16[256,2304]{1,0:T(8,128)(2,1)S(1)} %bitcast.5, f32[16,48,48]{2,1,0:T(8,128)S(1)} %bitcast.6, f32[16,48]{1,0:T(8,128)S(1)} %copy-done.8), custom_call_target="tpu_custom_call" | custom-call | tf_op jit(solution)/shard_map/query_gradient/pallas_call | solution.py:211
  46.2 9.6 %all_to_all.27.heard = bf16[8,8,128]{2,1,0:T(8,128)(2,1)S(1)} all-to-all(bf16[8,8,128]{2,1,0:T(8,128)(2,1)S(1)} %get-tuple-element.7), channel_id=1, replica_groups=mesh['zl'=4,'core'=2,'x'=4,'zh'=4,'y'=4] {'zl','core'}, dimensions={0} | all-to-all | bytes 32768 | tf_op jit(solution)/shard_map/all_to_all | solution.py:217
  55.8 0.0 copy-done.4
  55.8 0.0 copy-done.7
  55.8 0.0 copy-start.3
  55.8 0.3 lower_block.1
  56.0 0.0 copy-start.1
  56.1 8.2 %all_to_all.28.blocks = bf16[8,8,288]{2,1,0:T(8,128)(2,1)S(1)} all-to-all(bf16[8,8,288]{2,1,0:T(8,128)(2,1)S(1)} %lower_block.1), channel_id=1, replica_groups=mesh['zl'=4,'core'=2,'x'=4,'zh'=4,'y'=4] {'zl','core'}, dimensions={0} | all-to-all | bytes 73728 | tf_op jit(solution)/shard_map/all_to_all | solution.py:224
  64.3 0.2 build_message.1
  64.5 14.4 %all_to_all.29.message = bf16[16,8,2688]{2,1,0:T(8,128)(2,1)S(1)} all-to-all(bf16[16,8,2688]{2,1,0:T(8,128)(2,1)S(1)} %build_message.1), channel_id=1, replica_groups=mesh['zl'=4,'core'=2,'x'=4,'zh'=4,'y'=4] {'x','y'}, dimensions={0} | all-to-all | bytes 1376256 | tf_op jit(solution)/shard_map/all_to_all | solution.py:229
  78.9 0.0 copy-done.5
  78.9 0.0 copy-done.3
  78.9 0.0 copy-done.1
  79.0 2.4 %score.1 = f32[16,48,192]{2,1,0:T(8,128)} custom-call(s32[16]{0:T(128)S(1)} %copy-done.9, bf16[16,8,2688]{2,1,0:T(8,128)(2,1)S(1)} %all_to_all.29.message, bf16[2,192,2304]{2,1,0:T(8,128)(2,1)S(1)} %copy-done.1, bf16[16,48,192]{2,1,0:T(8,128)(2,1)S(1)} %copy-done.5, s32[16,48,192]{2,1,0:T(8,128)S(1)} %copy-done.3), custom_call_target="tpu_custom_call" | custom-call | tf_op jit(solution)/shard_map/score/pallas_call | solution.py:230
  (1 shorter events, 0.0 us)
Async XLA Ops:
  0.0 1.3 %copy-start = (bf16[250,2304]{1,0:T(8,128)(2,1)S(1)}, bf16[250,2304]{1,0:T(8,128)(2,1)}, u32[]{:S(2)}) copy-start(bf16[250,2304]{1,0:T(8,128)(2,1)} %param.13) | copy-start | bytes 3456004
  0.0 45.2 %copy-start.9 = (s32[16]{0:T(128)S(1)}, s32[16]{0:T(128)}, u32[]{:S(2)}) copy-start(s32[16]{0:T(128)} %position.3) | copy-start | bytes 196
  0.0 45.2 %copy-start.2 = (bf16[1,256,2304]{2,1,0:T(8,128)(2,1)S(1)}, bf16[1,256,2304]{2,1,0:T(8,128)(2,1)}, u32[]{:S(2)}) copy-start(bf16[1,256,2304]{2,1,0:T(8,128)(2,1)} %param.18) | copy-start | bytes 3538948
  0.0 45.2 %copy-start.8 = (f32[16,48]{1,0:T(8,128)S(1)}, f32[16,48]{1,0:T(8,128)}, u32[]{:S(2)}) copy-start(f32[16,48]{1,0:T(8,128)} %inv_rms.1) | copy-start | bytes 9220
  0.0 45.2 %copy-start.6 = (f32[1,16,48,48]{3,2,1,0:T(8,128)S(1)}, f32[1,16,48,48]{3,2,1,0:T(8,128)}, u32[]{:S(2)}) copy-start(f32[1,16,48,48]{3,2,1,0:T(8,128)} %param.14) | copy-start | bytes 442372
  2.4 53.4 %copy-start.4 = (bf16[4,288,256]{2,1,0:T(8,128)(2,1)S(1)}, bf16[4,288,256]{2,1,0:T(8,128)(2,1)}, u32[]{:S(2)}) copy-start(bf16[4,288,256]{2,1,0:T(8,128)(2,1)} %w_value.1) | copy-start | bytes 1769476
  2.4 53.4 %copy-start.7 = (f32[2304]{0:T(1024)S(1)}, f32[2304]{0:T(1024)}, u32[]{:S(2)}) copy-start(f32[2304]{0:T(1024)} %gain.1) | copy-start | bytes 27652
  45.3 33.7 %copy-start.5 = (bf16[16,48,192]{2,1,0:T(8,128)(2,1)S(1)}, bf16[16,48,192]{2,1,0:T(8,128)(2,1)}, u32[]{:S(2)}) copy-start(bf16[16,48,192]{2,1,0:T(8,128)(2,1)} %activation.1) | copy-start | bytes 884740
  55.8 23.2 %copy-start.3 = (s32[16,48,192]{2,1,0:T(8,128)S(1)}, s32[16,48,192]{2,1,0:T(8,128)}, u32[]{:S(2)}) copy-start(s32[16,48,192]{2,1,0:T(8,128)} %active.1) | copy-start | bytes 1769476
  56.0 22.9 %copy-start.1 = (bf16[2,192,2304]{2,1,0:T(8,128)(2,1)S(1)}, bf16[2,192,2304]{2,1,0:T(8,128)(2,1)}, u32[]{:S(2)}) copy-start(bf16[2,192,2304]{2,1,0:T(8,128)(2,1)} %decoder.1) | copy-start | bytes 5308420
